TPU v7x, 32 devices: a whole 2x2x4 slice. The times are simulated.
32 devices in a mesh: shard: 8 (over y, x, core), rep: 4 (over z).
Axes of the slice: x: 2, y: 2, z: 4, core: 2. Of those that a mesh axis runs over, the one named last changes fastest.
Arguments:
- tokens: bfloat16 [8, 1024, 2048], P('rep', 'shard'), may hold values from -6 to 6
- lengths: int32 [8], P('rep'), may hold values from 256 to 1024, as said below
- slot_adapter_index: int32 [8], P('rep'), may hold values from 0 to 7
- norm_gain_rows: float32 [2, 2048], replicated, may hold values from 0.1 to 1.9
- norm_shift_rows: float32 [2, 2048], replicated, may hold values from -1.75 to 1.75
- query_key_value_weight: bfloat16 [2048, 6144], P('shard'), may hold values from -0.125 to 0.125
- query_key_value_bias: float32 [6144], replicated, may hold values from -3 to 3
- output_projection_weight: bfloat16 [2048, 2048], P('shard'), may hold values from -0.25 to 0.25
- gate_up_projection: bfloat16 [5632, 2, 2048], P('shard'), may hold values from -0.125 to 0.125
- down_projection_weight: bfloat16 [5632, 2048], P('shard'), may hold values from -0.078125 to 0.078125
- attention_adapter_input: bfloat16 [2048, 384], P('shard'), may hold values from -0.125 to 0.125
- attention_adapter_output: bfloat16 [3, 128, 2048], P(None, None, 'shard'), may hold values from -0.375 to 0.375
- output_adapter_input: bfloat16 [2048, 128], P('shard'), may hold values from -0.125 to 0.125
- output_adapter_output: bfloat16 [128, 2048], P(None, 'shard'), may hold values from -0.375 to 0.375
- feedforward_adapter_input: bfloat16 [2048, 256], P('shard'), may hold values from -0.125 to 0.125
- feedforward_adapter_output: bfloat16 [5632, 2, 128], P('shard'), may hold values from -0.375 to 0.375
- down_adapter_input: bfloat16 [5632, 128], P('shard'), may hold values from -0.078125 to 0.078125
- down_adapter_output: bfloat16 [128, 2048], P(None, 'shard'), may hold values from -0.375 to 0.375
- output_cotangent: bfloat16 [8, 1024, 2048], P('rep', 'shard'), may hold values from -6 to 6
Outputs:
- block_out: bfloat16 [8, 1024, 2048], P('rep', 'shard')
- tokens_grad: float32 [8, 1024, 2048], P('rep', 'shard')
- qkv_lora_a_grad: float32 [2048, 384], P('shard')
- qkv_lora_b_grad: float32 [3, 128, 2048], P(None, None, 'shard')
- out_lora_a_grad: float32 [2048, 128], P('shard')
- out_lora_b_grad: float32 [128, 2048], P(None, 'shard')
- mlp_lora_a_grad: float32 [2048, 256], P('shard')
- mlp_lora_b_grad: float32 [5632, 2, 128], P('shard')
- down_lora_a_grad: float32 [5632, 128], P('shard')
- down_lora_b_grad: float32 [128, 2048], P(None, 'shard')
Inputs may be any that keep to these rules, and one draw needn't show every extreme that they name: `lengths`: in every draw some slot holds exactly 1024 tokens and some exactly 256.
All inputs are finite; a program needn't handle non-finite values.
Results may differ from a plain program's by a relative error of at most 0.022.
Values may be sent and summed in bfloat16 or wider, within the bound.
No kernel may reach another device: no remote copies, remote signals or barrier semaphores. Data moves between devices by JAX's collectives and lax.ppermute only.
A program may use at most 448 MiB of HBM per device.

v0:
```python
import math

import jax
import jax.numpy as jnp
from jax import lax
from jax.sharding import PartitionSpec as P

MODEL_WIDTH = 2048
HEADS = 32
HEAD_DIM = 64
ROT = 16
ADAPTER_COUNT = 8
ADAPTER_RANK = 16


adapter_scale = 2.0
norm_epsilon = 1e-05
rotary_base = 10000.0
masked_score = -1e30


def matrix_product(factor, partner):
    return jnp.dot(factor, partner, preferred_element_type=jnp.float32)


def matrix_product_transposed_right(factor, partner):
    return lax.dot_general(
        factor, partner, (((1,), (1,)), ((), ())), preferred_element_type=jnp.float32
    )


def matrix_product_transposed_left(factor, partner):
    return lax.dot_general(
        factor, partner, (((0,), (0,)), ((), ())), preferred_element_type=jnp.float32
    )


def layer_norm(values, gain_row, shift_row):
    average = jnp.mean(values, axis=-1, keepdims=True)
    centered = values - average
    variance = jnp.mean(centered * centered, axis=-1, keepdims=True)
    inverse = lax.rsqrt(variance + norm_epsilon)
    unit_rows = centered * inverse
    return (unit_rows * gain_row + shift_row, unit_rows, inverse)


def layer_norm_back(grad_rows, unit_rows, inverse, gain_row):
    scaled = grad_rows * gain_row
    return inverse * (
        scaled
        - jnp.mean(scaled, axis=-1, keepdims=True)
        - unit_rows * jnp.mean(scaled * unit_rows, axis=-1, keepdims=True)
    )


def rotary_tables(places):
    half_rot = ROT // 2
    spacing = jnp.arange(half_rot, dtype=jnp.float32) * (-2.0 * math.log(rotary_base) / ROT)
    turn_angles = places.astype(jnp.float32)[:, None] * jnp.exp(spacing)[None, :]
    return (jnp.cos(turn_angles), jnp.sin(turn_angles))


def rotate(values, cosine_table, sine_table):
    half_rot = ROT // 2
    former = values[..., :half_rot]
    latter = values[..., half_rot:ROT]
    cos_rows = cosine_table[:, None, :]
    sin_rows = sine_table[:, None, :]
    return jnp.concatenate(
        [
            former * cos_rows - latter * sin_rows,
            latter * cos_rows + former * sin_rows,
            values[..., ROT:],
        ],
        axis=-1,
    )


def adapter_forward(layer_inputs, down_mat, up_mat, select_adapter_rows, part_count, pattern):
    row_count = layer_inputs.shape[0]
    middle = (
        matrix_product(layer_inputs, down_mat).reshape(row_count, part_count, -1)
        * select_adapter_rows[:, None, :]
    )
    middle = middle.astype(jnp.bfloat16)
    return (jnp.einsum(pattern, middle, up_mat, preferred_element_type=jnp.float32), middle)


def adapter_down_back(middle_gradient, layer_inputs, down_mat, select_adapter_rows):
    mid_low = (
        middle_gradient.astype(jnp.bfloat16) * select_adapter_rows[:, None, :].astype(jnp.bfloat16)
    ).reshape(layer_inputs.shape[0], -1)
    return (
        matrix_product_transposed_right(mid_low, down_mat),
        matrix_product_transposed_left(layer_inputs, mid_low),
    )


def adapter_backward(grad_low, layer_inputs, middle, down_mat, up_mat, select_adapter_rows):
    up_gradient = adapter_scale * jnp.einsum(
        "tjr,tjd->jrd", middle, grad_low, preferred_element_type=jnp.float32
    )
    middle_gradient = adapter_scale * jnp.einsum(
        "tjd,jrd->tjr", grad_low, up_mat, preferred_element_type=jnp.float32
    )
    input_grad, down_grad = adapter_down_back(
        middle_gradient, layer_inputs, down_mat, select_adapter_rows
    )
    return (input_grad, down_grad, up_gradient)


def gate_backward(gate_cols, hidden_grad):
    gate_part = gate_cols[:, 0]
    up_part = gate_cols[:, 1]
    sigmoid = jax.nn.sigmoid(gate_part)
    silu_vals = gate_part * sigmoid
    gated_hidden = (silu_vals * up_part).astype(jnp.bfloat16)
    gate_grad = hidden_grad * up_part * sigmoid * (1.0 + gate_part * (1.0 - sigmoid))
    up_gradient = hidden_grad * silu_vals
    return (jnp.stack([gate_grad, up_gradient], axis=1).astype(jnp.bfloat16), gated_hidden)


def head_mask(query_places, key_places, lengths):
    return (key_places[None, None, None, :] <= query_places[None, :, None, None]) & (
        key_places[None, None, None, :] < lengths[:, None, None, None]
    )


def head_forward(head_queries, head_keys, head_values, lengths):
    span = head_queries.shape[1]
    block_rows = min(512, span)
    key_places = jnp.arange(span, dtype=jnp.int32)
    score_scale = HEAD_DIM ** (-0.5)
    outputs = []
    totals = []
    for first_row in range(0, span, block_rows):
        query_block = head_queries[:, first_row : first_row + block_rows]
        query_places = first_row + jnp.arange(block_rows, dtype=jnp.int32)
        scores = (
            jnp.einsum(
                "sqgd,skgd->sqgk", query_block, head_keys, preferred_element_type=jnp.float32
            )
            * score_scale
        )
        scores = jnp.where(head_mask(query_places, key_places, lengths), scores, masked_score)
        top = jnp.max(scores, axis=-1, keepdims=True)
        shifted = jnp.exp(scores - top)
        total = jnp.sum(shifted, axis=-1, keepdims=True)
        probabilities = shifted / total
        outputs.append(
            jnp.einsum(
                "sqgk,skgd->sqgd",
                probabilities.astype(jnp.bfloat16),
                head_values,
                preferred_element_type=jnp.float32,
            )
        )
        totals.append((top + jnp.log(total))[..., 0])
    return (jnp.concatenate(outputs, axis=1), jnp.concatenate(totals, axis=1))


def head_backward(
    head_queries, head_keys, head_values, head_lse, head_attended, head_dout, lengths
):
    span = head_queries.shape[1]
    block_rows = min(512, span)
    key_places = jnp.arange(span, dtype=jnp.int32)
    score_scale = HEAD_DIM ** (-0.5)
    delta_rows = jnp.sum(head_dout.astype(jnp.float32) * head_attended, axis=-1)
    query_parts = []
    key_sum = jnp.zeros(head_keys.shape, jnp.float32)
    value_sum = jnp.zeros(head_values.shape, jnp.float32)
    for first_row in range(0, span, block_rows):
        query_block = head_queries[:, first_row : first_row + block_rows]
        dout_block = head_dout[:, first_row : first_row + block_rows]
        query_places = first_row + jnp.arange(block_rows, dtype=jnp.int32)
        scores = (
            jnp.einsum(
                "sqgd,skgd->sqgk", query_block, head_keys, preferred_element_type=jnp.float32
            )
            * score_scale
        )
        allowed = head_mask(query_places, key_places, lengths)
        probabilities = jnp.where(
            allowed, jnp.exp(scores - head_lse[:, first_row : first_row + block_rows, :, None]), 0.0
        )
        prob_grad = jnp.einsum(
            "sqgd,skgd->sqgk", dout_block, head_values, preferred_element_type=jnp.float32
        )
        score_grad = (
            probabilities * (prob_grad - delta_rows[:, first_row : first_row + block_rows, :, None])
        ).astype(jnp.bfloat16)
        query_parts.append(
            score_scale
            * jnp.einsum(
                "sqgk,skgd->sqgd", score_grad, head_keys, preferred_element_type=jnp.float32
            )
        )
        key_sum = key_sum + score_scale * jnp.einsum(
            "sqgk,sqgd->skgd", score_grad, query_block, preferred_element_type=jnp.float32
        )
        value_sum = value_sum + jnp.einsum(
            "sqgk,sqgd->skgd",
            probabilities.astype(jnp.bfloat16),
            dout_block,
            preferred_element_type=jnp.float32,
        )
    return (jnp.concatenate(query_parts, axis=1), key_sum, value_sum)


def per_device(
    tokens,
    lengths,
    slot_adapter_index,
    norm_gain_rows,
    norm_shift_rows,
    query_key_value_weight,
    query_key_value_bias,
    output_projection_weight,
    gate_up_projection,
    down_projection_weight,
    attention_adapter_input,
    attention_adapter_output,
    output_adapter_input,
    output_adapter_output,
    feedforward_adapter_input,
    feedforward_adapter_output,
    down_adapter_input,
    down_adapter_output,
    output_cotangent,
):
    slot_count, local_span = (tokens.shape[0], tokens.shape[1])
    row_count = slot_count * local_span
    offset = lax.axis_index("shard") * local_span
    places = offset + jnp.arange(local_span, dtype=jnp.int32)
    valid_rows = (places[None, :] < lengths[:, None]).astype(jnp.float32).reshape(row_count, 1)
    columns = ADAPTER_COUNT * ADAPTER_RANK
    choose = (
        jnp.arange(columns, dtype=jnp.int32)[None, :] // ADAPTER_RANK == slot_adapter_index[:, None]
    ).astype(jnp.float32)
    select_adapter_rows = jnp.broadcast_to(
        choose[:, None, :], (slot_count, local_span, columns)
    ).reshape(row_count, columns)
    gathered = (
        lax.all_gather(query_key_value_weight, "shard", axis=0, tiled=True),
        lax.all_gather(output_projection_weight, "shard", axis=0, tiled=True),
        lax.all_gather(attention_adapter_input, "shard", axis=0, tiled=True),
        lax.all_gather(attention_adapter_output, "shard", axis=2, tiled=True),
        lax.all_gather(output_adapter_input, "shard", axis=0, tiled=True),
        lax.all_gather(output_adapter_output, "shard", axis=1, tiled=True),
        lax.all_gather(feedforward_adapter_input, "shard", axis=0, tiled=True),
        lax.all_gather(feedforward_adapter_output, "shard", axis=0, tiled=True),
        lax.all_gather(down_adapter_input, "shard", axis=0, tiled=True),
        lax.all_gather(down_adapter_output, "shard", axis=1, tiled=True),
    )
    (
        qkv_full,
        output_complete,
        attention_input_map,
        attention_output_map,
        output_input_map,
        output_output_map,
        feedforward_input_map,
        feedforward_output_map,
        down_input_map,
        down_output_map,
    ) = gathered
    layer_inputs = tokens.reshape(row_count, MODEL_WIDTH).astype(jnp.float32)
    first_normalized, unit_one, inverse_one = layer_norm(
        layer_inputs, norm_gain_rows[0], norm_shift_rows[0]
    )
    normed_low = first_normalized.astype(jnp.bfloat16)
    projected_rows = matrix_product(normed_low, qkv_full).reshape(
        row_count, 3, MODEL_WIDTH
    ) + query_key_value_bias.reshape(3, MODEL_WIDTH)
    adapter_update, qkv_middle = adapter_forward(
        normed_low,
        attention_input_map,
        attention_output_map,
        select_adapter_rows,
        3,
        "wsq,sql->wsl",
    )
    projected_rows = projected_rows + adapter_scale * adapter_update
    cosine_table, sine_table = rotary_tables(places)
    shaped = projected_rows.reshape(slot_count, local_span, 3, HEADS, HEAD_DIM)
    queries = rotate(shaped[:, :, 0], cosine_table, sine_table).astype(jnp.bfloat16)
    keys_here = rotate(shaped[:, :, 1], cosine_table, sine_table).astype(jnp.bfloat16)
    values_here = shaped[:, :, 2].astype(jnp.bfloat16)
    head_queries, head_keys, head_values = (
        lax.all_to_all(queries, "shard", split_axis=2, concat_axis=1, tiled=True),
        lax.all_to_all(keys_here, "shard", split_axis=2, concat_axis=1, tiled=True),
        lax.all_to_all(values_here, "shard", split_axis=2, concat_axis=1, tiled=True),
    )
    head_attended, head_lse = head_forward(head_queries, head_keys, head_values, lengths)
    attention_output_reduced = lax.all_to_all(
        head_attended.astype(jnp.bfloat16), "shard", split_axis=1, concat_axis=2, tiled=True
    ).reshape(row_count, MODEL_WIDTH)
    adapter_update, out_middle = adapter_forward(
        attention_output_reduced,
        output_input_map,
        output_output_map[None],
        select_adapter_rows,
        1,
        "wsq,sql->wsl",
    )
    hidden_input_rows = layer_inputs + (
        matrix_product(attention_output_reduced, output_complete)
        + adapter_scale * adapter_update[:, 0]
    )
    second_normalized, unit_two, inverse_two = layer_norm(
        hidden_input_rows, norm_gain_rows[1], norm_shift_rows[1]
    )
    normed_two_low = second_normalized.astype(jnp.bfloat16)
    second_middle = (
        matrix_product(normed_two_low, feedforward_input_map).reshape(row_count, 2, columns)
        * select_adapter_rows[:, None, :]
    ).astype(jnp.bfloat16)
    gate_piece = lax.all_gather(gate_up_projection, "shard", axis=0, tiled=True)
    down_piece = lax.all_gather(down_projection_weight, "shard", axis=0, tiled=True)
    adapter_piece = feedforward_output_map
    gate_cols = jnp.einsum(
        "td,fjd->tjf", normed_two_low, gate_piece, preferred_element_type=jnp.float32
    ) + adapter_scale * jnp.einsum(
        "ilz,plz->ilp", second_middle, adapter_piece, preferred_element_type=jnp.float32
    )
    gated_hidden = (jax.nn.silu(gate_cols[:, 0]) * gate_cols[:, 1]).astype(jnp.bfloat16)
    down_total = matrix_product(gated_hidden, down_piece)
    mid_sum = matrix_product(gated_hidden, down_input_map)
    gate_store = gate_cols
    third_middle_reduced = (mid_sum * select_adapter_rows).astype(jnp.bfloat16)
    feedforward_output = down_total + adapter_scale * matrix_product(
        third_middle_reduced, down_output_map
    )
    block_out = (
        ((hidden_input_rows + feedforward_output) * valid_rows)
        .astype(jnp.bfloat16)
        .reshape(slot_count, local_span, MODEL_WIDTH)
    )
    grad_rows = output_cotangent.reshape(row_count, MODEL_WIDTH).astype(jnp.float32) * valid_rows
    feedforward_reduced = grad_rows.astype(jnp.bfloat16)
    down_output_map_gradient = adapter_scale * matrix_product_transposed_left(
        third_middle_reduced, feedforward_reduced
    )
    third_middle_gradient = (
        adapter_scale * matrix_product_transposed_right(feedforward_reduced, down_output_map)
    ).astype(jnp.bfloat16) * select_adapter_rows.astype(jnp.bfloat16)
    gate_piece = lax.all_gather(gate_up_projection, "shard", axis=0, tiled=True)
    down_piece = lax.all_gather(down_projection_weight, "shard", axis=0, tiled=True)
    adapter_piece = feedforward_output_map
    gate_cols = gate_store
    hidden_grad = matrix_product_transposed_right(
        feedforward_reduced, down_piece
    ) + matrix_product_transposed_right(third_middle_gradient, down_input_map)
    gate_gradient_reduced, gated_hidden = gate_backward(gate_cols, hidden_grad)
    input_sum = jnp.einsum(
        "tjf,fjd->td", gate_gradient_reduced, gate_piece, preferred_element_type=jnp.float32
    )
    middle_total = adapter_scale * jnp.einsum(
        "lnh,hnu->lnu", gate_gradient_reduced, adapter_piece, preferred_element_type=jnp.float32
    )
    adapter_store = adapter_scale * jnp.einsum(
        "tjr,tjf->fjr", second_middle, gate_gradient_reduced, preferred_element_type=jnp.float32
    )
    down_store = matrix_product_transposed_left(gated_hidden, third_middle_gradient)
    mlp_input_grad, mlp_a_grad = adapter_down_back(
        middle_total, normed_two_low, feedforward_input_map, select_adapter_rows
    )
    residual_grad = grad_rows + layer_norm_back(
        input_sum + mlp_input_grad, unit_two, inverse_two, norm_gain_rows[1]
    )
    branch_low = residual_grad.astype(jnp.bfloat16)
    qkv_back, out_back = (qkv_full, output_complete)
    attended_part, out_a_grad, out_b_grad = adapter_backward(
        branch_low[:, None, :],
        attention_output_reduced,
        out_middle,
        output_input_map,
        output_output_map[None],
        select_adapter_rows,
    )
    attended_grad = (matrix_product_transposed_right(branch_low, out_back) + attended_part).astype(
        jnp.bfloat16
    )
    dout_heads = attended_grad.reshape(slot_count, local_span, HEADS, HEAD_DIM)
    head_dout = lax.all_to_all(dout_heads, "shard", split_axis=2, concat_axis=1, tiled=True)
    head_query_grad, head_key_grad, head_value_grad = head_backward(
        head_queries, head_keys, head_values, head_lse, head_attended, head_dout, lengths
    )
    query_grad, key_grad, value_grad = (
        lax.all_to_all(
            head_query_grad.astype(jnp.bfloat16), "shard", split_axis=1, concat_axis=2, tiled=True
        ).astype(head_query_grad.dtype),
        lax.all_to_all(
            head_key_grad.astype(jnp.bfloat16), "shard", split_axis=1, concat_axis=2, tiled=True
        ).astype(head_key_grad.dtype),
        lax.all_to_all(
            head_value_grad.astype(jnp.bfloat16), "shard", split_axis=1, concat_axis=2, tiled=True
        ).astype(head_value_grad.dtype),
    )
    key_grad = key_grad.reshape(slot_count, local_span, MODEL_WIDTH)
    value_grad = value_grad.reshape(slot_count, local_span, MODEL_WIDTH)
    unused_out, unturn = jax.vjp(
        lambda turned: rotate(turned, cosine_table, sine_table),
        jnp.zeros((slot_count, local_span, HEADS, HEAD_DIM), jnp.float32),
    )
    query_plain = unturn(query_grad)[0].reshape(row_count, MODEL_WIDTH)
    key_plain = unturn(key_grad.reshape(slot_count, local_span, HEADS, HEAD_DIM))[0].reshape(
        row_count, MODEL_WIDTH
    )
    projected_grad = jnp.stack(
        [query_plain, key_plain, value_grad.reshape(row_count, MODEL_WIDTH)], axis=1
    ).astype(jnp.bfloat16)
    normed_part, qkv_a_grad, qkv_b_grad = adapter_backward(
        projected_grad,
        normed_low,
        qkv_middle,
        attention_input_map,
        attention_output_map,
        select_adapter_rows,
    )
    normed_grad = (
        matrix_product_transposed_right(
            projected_grad.reshape(row_count, 3 * MODEL_WIDTH), qkv_back
        )
        + normed_part
    )
    tokens_grad = (
        residual_grad + layer_norm_back(normed_grad, unit_one, inverse_one, norm_gain_rows[0])
    ).reshape(slot_count, local_span, MODEL_WIDTH)
    owner_sums = (
        lax.psum_scatter(
            qkv_a_grad.astype(jnp.bfloat16), "shard", scatter_dimension=0, tiled=True
        ).astype(jnp.float32),
        lax.psum_scatter(
            qkv_b_grad.astype(jnp.bfloat16), "shard", scatter_dimension=2, tiled=True
        ).astype(jnp.float32),
        lax.psum_scatter(
            out_a_grad.astype(jnp.bfloat16), "shard", scatter_dimension=0, tiled=True
        ).astype(jnp.float32),
        lax.psum_scatter(
            out_b_grad[0].astype(jnp.bfloat16), "shard", scatter_dimension=1, tiled=True
        ).astype(jnp.float32),
        lax.psum_scatter(
            mlp_a_grad.astype(jnp.bfloat16), "shard", scatter_dimension=0, tiled=True
        ).astype(jnp.float32),
        lax.psum_scatter(
            adapter_store.astype(jnp.bfloat16), "shard", scatter_dimension=0, tiled=True
        ).astype(jnp.float32),
        lax.psum_scatter(
            down_store.astype(jnp.bfloat16), "shard", scatter_dimension=0, tiled=True
        ).astype(jnp.float32),
        lax.psum_scatter(
            down_output_map_gradient.astype(jnp.bfloat16), "shard", scatter_dimension=1, tiled=True
        ).astype(jnp.float32),
    )
    summed = (
        lax.psum(owner_sums[0].astype(jnp.bfloat16), "rep").astype(jnp.float32),
        lax.psum(owner_sums[1].astype(jnp.bfloat16), "rep").astype(jnp.float32),
        lax.psum(owner_sums[2].astype(jnp.bfloat16), "rep").astype(jnp.float32),
        lax.psum(owner_sums[3].astype(jnp.bfloat16), "rep").astype(jnp.float32),
        lax.psum(owner_sums[4].astype(jnp.bfloat16), "rep").astype(jnp.float32),
        lax.psum(owner_sums[5].astype(jnp.bfloat16), "rep").astype(jnp.float32),
        lax.psum(owner_sums[6].astype(jnp.bfloat16), "rep").astype(jnp.float32),
        lax.psum(owner_sums[7].astype(jnp.bfloat16), "rep").astype(jnp.float32),
    )
    return (
        block_out,
        tokens_grad,
        summed[0],
        summed[1],
        summed[2],
        summed[3],
        summed[4],
        summed[5],
        summed[6],
        summed[7],
    )


def solution(mesh):
    in_specs = (
        P("rep", "shard", None),
        P("rep"),
        P("rep"),
        P(),
        P(),
        P("shard", None),
        P(),
        P("shard", None),
        P("shard", None, None),
        P("shard", None),
        P("shard", None),
        P(None, None, "shard"),
        P("shard", None),
        P(None, "shard"),
        P("shard", None),
        P("shard", None, None),
        P("shard", None),
        P(None, "shard"),
        P("rep", "shard", None),
    )
    out_specs = (
        P("rep", "shard", None),
        P("rep", "shard", None),
        P("shard", None),
        P(None, None, "shard"),
        P("shard", None),
        P(None, "shard"),
        P("shard", None),
        P("shard", None, None),
        P("shard", None),
        P(None, "shard"),
    )
    return jax.shard_map(
        per_device, mesh=mesh, in_specs=in_specs, out_specs=out_specs, check_vma=False
    )
```

profile of v0, /device:TPU:0, one launch (start us, length us, event | category | flops | bytes accessed | tf_op | source)
XLA Modules:
  0.0 1166.5 jit_solution(10940483634782380386)
XLA Ops:
  11.2 7.8 copy.97
  26.9 13.2 %all_gather.42 = bf16[2048,128]{1,0:T(8,128)(2,1)} all-gather(bf16[256,128]{1,0:T(8,128)(2,1)S(1)} %copy-done.55), channel_id=1, replica_groups=mesh['shard'=8,'rep'=4] {'shard'}, dimensions={0}, use_global_device_ids=true | all-gather | bytes 589824 | tf_op jit(solution)/shard_map/all_gather | solution.py:249
  40.8 12.3 %all_gather.49 = bf16[128,2048]{1,0:T(8,128)(2,1)} all-gather(bf16[128,256]{1,0:T(8,128)(2,1)S(1)} %copy-done.56), channel_id=1, replica_groups=mesh['shard'=8,'rep'=4] {'shard'}, dimensions={1}, use_global_device_ids=true | all-gather | bytes 589824 | tf_op jit(solution)/shard_map/all_gather | solution.py:254
  59.6 107.0 %all-gather.10.cloned.1.call-done = bf16[2048,6144]{1,0:T(8,128)(2,1)} async-done(((bf16[256,6144]{1,0:T(8,128)(2,1)}), bf16[2048,6144]{1,0:T(8,128)(2,1)}) %all-gather.10.cloned.1.call-update) | async-done | bytes 25165840 | tf_op jit(solution)/shard_map/all_gather | solution.py:245
  166.6 29.7 %copy.87 = bf16[6144,2048]{1,0:T(8,128)(2,1)} copy(bf16[6144,2048]{0,1:T(8,128)(2,1)} %bitcast.329) | data formatting | bytes 50331648 | tf_op jit(solution)/shard_map/dot_general | solution.py:23
  196.4 15.7 %fusion.118 = f32[256,3,2048]{2,0,1:T(8,128)} fusion(bf16[256,2048,1]{1,0,2:T(8,128)(2,1)S(1)} %bitcast.331, bf16[3,2048,2048]{2,1,0:T(8,128)(2,1)} %bitcast.325), kind=kOutput, calls=%fused_computation.220 | convolution fusion | flops 6442450944 | bytes 32505856 | tf_op jit(solution)/shard_map/dot_general | solution.py:23
  225.7 8.3 reshape.492
  252.6 18.8 %all-to-all-done.2 = bf16[2,128,32,64]{1,0,3,2:T(2,128)(2,1)} async-done(((bf16[2,128,32,64]{1,0,3,2:T(2,128)(2,1)}), bf16[2,128,32,64]{1,0,3,2:T(2,128)(2,1)}, u32[]{:S(2)}, u32[]{:S(2)}) %all-to-all-start.2) | async-done | bytes 1048608 | tf_op jit(solution)/shard_map/all_to_all | solution.py:291
  275.0 34.4 %all_gather.43 = bf16[128,2048]{1,0:T(8,128)(2,1)} all-gather(bf16[128,256]{1,0:T(8,128)(2,1)S(1)} %copy-done.57), channel_id=1, replica_groups=mesh['shard'=8,'rep'=4] {'shard'}, dimensions={1}, use_global_device_ids=true | all-gather | bytes 589824 | tf_op jit(solution)/shard_map/all_gather | solution.py:250
  329.0 8.9 fusion.8
  337.8 7.4 fusion.9
  352.2 15.2 %fusion.10 = (f32[2,512,4]{1,2,0:T(4,128)S(1)}, f32[2,512,4]{1,2,0:T(4,128)S(1)}) fusion(f32[2,4,1024,512]{3,2,1,0:T(8,128)} %get-tuple-element.88, f32[2,512,4]{1,2,0:T(4,128)S(1)} %get-tuple-element.87, pred[2,512,1024]{1,2,0:T(8,128)(4,1)S(1)} %get-tuple-element.75, f32[2,512,4]{1,2,0:T(4,128)S(1)} %get-tuple-element.85, ...), kind=kLoop, calls=%fused_computation.20 | loop fusion | flops 33546240 | bytes 35717120 | tf_op jit(solution)/shard_map/reduce_sum | solution.py:148
  367.4 8.3 fusion.48
  392.5 13.4 %fusion.121 = f32[256,5632]{1,0:T(8,128)} fusion(bf16[256,2048]{1,0:T(8,128)(2,1)S(1)} %copy-done.15, bf16[5632,2048]{1,0:T(8,128)(2,1)} %all-gather.24.cloned.1.call-done), kind=kOutput, calls=%fused_computation.223 | convolution fusion | flops 5905580032 | bytes 29884416 | tf_op jit(solution)/shard_map/dot_general | solution.py:27
  428.6 9.5 all-gather.20.cloned.1.call-done
  441.7 212.4 %all-gather.18.cloned.1.call-done = bf16[5632,2,2048]{2,0,1:T(8,128)(2,1)} async-done(((bf16[704,2,2048]{2,0,1:T(8,128)(2,1)}), bf16[5632,2,2048]{2,0,1:T(8,128)(2,1)}) %all-gather.18.cloned.1.call-update) | async-done | bytes 46137360 | tf_op jit(solution)/shard_map/all_gather | solution.py:319
  654.1 23.5 %fusion.76 = f32[256,5632,2]{1,0,2:T(8,128)} fusion(bf16[5632,2,2048]{2,0,1:T(8,128)(2,1)} %all-gather.18.cloned.1.call-done, bf16[256,2048]{1,0:T(8,128)(2,1)S(1)} %add_convert_fusion.1), kind=kOutput, calls=%fused_computation.143 | convolution fusion | flops 11811160064 | bytes 58720256 | tf_op jit(solution)/shard_map/td,fjd->tjf/dot_general | solution.py:322
  677.6 10.0 all-gather.22.cloned.1.call-done
  687.6 11.1 bitcast_add_fusion
  698.7 15.9 %all-gather.26.cloned.1.call-done = bf16[5632,128]{1,0:T(8,128)(2,1)} async-done(((bf16[704,128]{1,0:T(8,128)(2,1)}), bf16[5632,128]{1,0:T(8,128)(2,1)}) %all-gather.26.cloned.1.call-update) | async-done | bytes 1441808 | tf_op jit(solution)/shard_map/all_gather | solution.py:253
  714.6 10.2 fusion.26
  724.8 23.4 %convolution_bitcast_fusion = f32[256,2048]{1,0:T(8,128)} fusion(bf16[5632,2,2048]{2,0,1:T(8,128)(2,1)} %all-gather.18.cloned.1.call-done, bf16[256,1,5632]{2,0,1:T(8,128)(2,1)} %get-tuple-element.53, bf16[256,1,5632]{2,0,1:T(8,128)(2,1)} %get-tuple-element.52), kind=kOutput, calls=%fused_computation.62 | convolution fusion | flops 11814043648 | bytes 54001664 | tf_op jit(solution)/shard_map/tjf,fjd->td/dot_general | solution.py:356
  792.9 9.3 all-to-all-done.4
  805.8 9.5 fusion.3
  821.6 9.3 fusion.1
  860.6 11.1 fusion.14
  875.9 11.3 fusion.50
  971.0 11.8 %fusion.120 = f32[256,2048]{1,0:T(8,128)S(1)} fusion(bf16[256,5632]{1,0:T(8,128)(2,1)} %get-tuple-element.54, bf16[5632,2048]{1,0:T(8,128)(2,1)} %all-gather.24.cloned.1.call-done), kind=kOutput, calls=%fused_computation.222 | convolution fusion | flops 5905580032 | bytes 28049408 | tf_op jit(solution)/shard_map/dot_general | solution.py:23
  989.0 13.9 %fusion.122 = f32[256,2048]{1,0:T(8,128)} fusion(bf16[256,6144]{0,1:T(8,128)(2,1)} %bitcast.356, bf16[2048,6144]{1,0:T(8,128)(2,1)} %all-gather.10.cloned.1.call-done), kind=kOutput, calls=%fused_computation.224 | convolution fusion | flops 6442450944 | bytes 30408704 | tf_op jit(solution)/shard_map/dot_general | solution.py:27
  1003.0 36.2 %reduce-scatter.9.cloned.1.call-done = bf16[256,384]{1,0:T(8,128)(2,1)} async-done(((bf16[2048,384]{1,0:T(8,128)(2,1)}), bf16[256,384]{1,0:T(8,128)(2,1)}) %reduce-scatter.9.cloned.1.call-update) | async-done | bytes 196624 | tf_op jit(solution)/shard_map/reduce_scatter | solution.py:432
  1039.2 48.0 %reduce-scatter.19.cloned.1.call-done = bf16[704,2,128]{2,0,1:T(8,128)(2,1)} async-done(((bf16[5632,2,128]{2,0,1:T(8,128)(2,1)}), bf16[704,2,128]{2,0,1:T(8,128)(2,1)}) %reduce-scatter.19.cloned.1.call-update) | async-done | bytes 360464 | tf_op jit(solution)/shard_map/reduce_scatter | solution.py:447
  1092.2 57.2 %all-reduce.9.cloned.1.call-done = (bf16[704,2,128]{2,0,1:T(8,128)(2,1)}, bf16[256,384]{1,0:T(8,128)(2,1)}, bf16[3,128,256]{2,1,0:T(8,128)(2,1)}, bf16[256,128]{...) async-done(((bf16[704,2,128]{2,0,1:T(8,128)(2,1)}, bf16[256,384]{1,0:T(8,128)(2,1)}, ...) | async-done | bytes 1261584 | tf_op jit(solution)/shard_map/psum | solution.py:463
  (361 shorter events, 316.9 us)
Async XLA Ops:
  7.2 47.3 %all-gather.12.cloned.1.call-start = ((), (), s32[]{:S(2)}) async-start(), calls=%async_computation.17 | async-start | bytes 1769472 | tf_op jit(solution)/shard_map/all_gather | solution.py:247
  7.9 158.7 %all-gather.10.cloned.1.call-start = ((), (), s32[]{:S(2)}) async-start(), calls=%async_computation.16 | async-start | bytes 28311552 | tf_op jit(solution)/shard_map/all_gather | solution.py:245
  8.7 203.4 %all-gather.14.cloned.1.call-start = ((), (), s32[]{:S(2)}) async-start(), calls=%async_computation.18 | async-start | bytes 1769472 | tf_op jit(solution)/shard_map/all_gather | solution.py:248
  9.4 383.1 %all-gather.24.cloned.1.call-start = ((), (), s32[]{:S(2)}) async-start(), calls=%async_computation.23 | async-start | bytes 25952256 | tf_op jit(solution)/shard_map/all_gather | solution.py:320
  10.0 411.2 %all-gather.16.cloned.1.call-start = ((), (), s32[]{:S(2)}) async-start(), calls=%async_computation.19 | async-start | bytes 9437184 | tf_op jit(solution)/shard_map/all_gather | solution.py:246
  10.6 427.6 %all-gather.20.cloned.1.call-start = ((), (), s32[]{:S(2)}) async-start(), calls=%async_computation.21 | async-start | bytes 1179648 | tf_op jit(solution)/shard_map/all_gather | solution.py:251
  11.1 642.9 %all-gather.18.cloned.1.call-start = ((), (), s32[]{:S(2)}) async-start(), calls=%async_computation.20 | async-start | bytes 51904512 | tf_op jit(solution)/shard_map/all_gather | solution.py:319
  19.1 668.6 %all-gather.22.cloned.1.call-start = ((), (), s32[]{:S(2)}) async-start(), calls=%async_computation.22 | async-start | bytes 3244032 | tf_op jit(solution)/shard_map/all_gather | solution.py:252
  20.8 693.8 %all-gather.26.cloned.1.call-start = ((), (), s32[]{:S(2)}) async-start(), calls=%async_computation.24 | async-start | bytes 1622016 | tf_op jit(solution)/shard_map/all_gather | solution.py:253
  40.2 204.6 %copy-start.69 = (f32[256]{0:T(256)}, f32[256]{0:T(256)S(1)}, u32[]{:S(2)}) copy-start(f32[256]{0:T(256)S(1)} %fusion.92) | copy-start | bytes 3076
  53.9 183.1 %copy-start.61 = (f32[128,8]{0,1:T(8,128)}, f32[128,8]{0,1:T(8,128)S(1)}, u32[]{:S(2)}) copy-start(f32[128,8]{0,1:T(8,128)S(1)} %get-tuple-element.83) | copy-start | bytes 12292
  53.9 183.1 %copy-start.63 = (f32[128,8]{0,1:T(8,128)}, f32[128,8]{0,1:T(8,128)S(1)}, u32[]{:S(2)}) copy-start(f32[128,8]{0,1:T(8,128)S(1)} %get-tuple-element.84) | copy-start | bytes 12292
  54.4 142.0 %copy-start.7 = (bf16[2,128,2048]{2,1,0:T(8,128)(2,1)}, bf16[2,128,2048]{2,1,0:T(8,128)(2,1)S(1)}, u32[]{:S(2)}) copy-start(bf16[2,128,2048]{2,1,0:T(8,128)(2,1)S(1)} %add_convert_fusion.2) | copy-start | bytes 3145732
  59.6 152.4 %copy-start.31 = (bf16[256,3,128]{2,0,1:T(8,128)(2,1)}, bf16[256,3,128]{2,0,1:T(8,128)(2,1)S(1)}, u32[]{:S(2)}) copy-start(bf16[256,3,128]{2,0,1:T(8,128)(2,1)S(1)} %fusion.57) | copy-start | bytes 589828
  240.5 30.9 %all-to-all-start.2 = ((bf16[2,128,32,64]{1,0,3,2:T(2,128)(2,1)}), bf16[2,128,32,64]{1,0,3,2:T(2,128)(2,1)}, u32[]{:S(2)}, u32[]{:S(2)}) async-start(bf16[2,128,32,64]{1,0,3,2:T(2,128)(2,1)} %pad_maximum_fusion.12), calls=%async_computation.2 | async-start | bytes 2097152 | tf_op jit(solution)/shard_map/all_to_all | solution.py:291
  271.4 50.1 %all-to-all-start.1 = ((bf16[2,128,32,64]{1,0,3,2:T(2,128)(2,1)}), bf16[2,128,32,64]{1,0,3,2:T(2,128)(2,1)S(1)}, u32[]{:S(2)}, u32[]{:S(2)}) async-start(bf16[2,128,32,64]{1,0,3,2:T(2,128)(2,1)} %pad_maximum_fusion.11), calls=%async_computation.1 | async-start | bytes 2097152 | tf_op jit(solution)/shard_map/all_to_all | solution.py:292
  321.5 25.5 %all-to-all-start = ((bf16[2,128,32,64]{1,0,3,2:T(2,128)(2,1)}), bf16[2,128,32,64]{1,0,3,2:T(2,128)(2,1)}, u32[]{:S(2)}, u32[]{:S(2)}) async-start(bf16[2,128,32,64]{1,0,3,2:T(2,128)(2,1)} %fusion.71), calls=%async_computation | async-start | bytes 2097152 | tf_op jit(solution)/shard_map/all_to_all | solution.py:293
  388.0 24.6 %all-to-all-start.3 = ((bf16[8,2,32768]{2,1,0:T(2,128)(2,1)}), bf16[8,2,32768]{2,1,0:T(2,128)(2,1)}, u32[]{:S(2)}, u32[]{:S(2)}) async-start(bf16[8,2,32768]{2,1,0:T(2,128)(2,1)} %reshape.513), calls=%async_computation.3 | async-start | bytes 2097152 | tf_op jit(solution)/shard_map/all_to_all | solution.py:296
  392.3 610.6 %reduce-scatter.15.cloned.1.call-start = ((), (), s32[]{:S(2)}) async-start(), calls=%async_computation.28 | async-start | bytes 589824 | tf_op jit(solution)/shard_map/reduce_scatter | solution.py:441
  758.5 244.4 %reduce-scatter.13.cloned.1.call-start = ((), (), s32[]{:S(2)}) async-start(), calls=%async_computation.27 | async-start | bytes 589824 | tf_op jit(solution)/shard_map/reduce_scatter | solution.py:438
  764.4 238.6 %reduce-scatter.23.cloned.1.call-start = ((), (), s32[]{:S(2)}) async-start(), calls=%async_computation.32 | async-start | bytes 589824 | tf_op jit(solution)/shard_map/reduce_scatter | solution.py:453
  769.7 233.3 %reduce-scatter.17.cloned.1.call-start = ((), (), s32[]{:S(2)}) async-start(), calls=%async_computation.29 | async-start | bytes 1179648 | tf_op jit(solution)/shard_map/reduce_scatter | solution.py:444
  782.6 19.6 %all-to-all-start.4 = ((bf16[2,128,32,64]{1,0,3,2:T(2,128)(2,1)}), bf16[2,128,32,64]{1,0,3,2:T(2,128)(2,1)S(1)}, u32[]{:S(2)}, u32[]{:S(2)}) async-start(bf16[2,128,32,64]{1,0,3,2:T(2,128)(2,1)} %reshape.498), calls=%async_computation.4 | async-start | bytes 2097152 | tf_op jit(solution)/shard_map/all_to_all | solution.py:386
  786.1 216.8 %reduce-scatter.21.cloned.1.call-start = ((), (), s32[]{:S(2)}) async-start(), calls=%async_computation.31 | async-start | bytes 1622016 | tf_op jit(solution)/shard_map/reduce_scatter | solution.py:450
  845.3 26.3 %all-to-all-start.6 = ((bf16[8,2,32768]{2,1,0:T(2,128)(2,1)}), bf16[8,2,32768]{2,1,0:T(2,128)(2,1)}, u32[]{:S(2)}, u32[]{:S(2)}) async-start(bf16[8,2,32768]{2,1,0:T(2,128)(2,1)} %reshape.517), calls=%async_computation.6 | async-start | bytes 2097152 | tf_op jit(solution)/shard_map/all_to_all | solution.py:394
  871.7 24.0 %all-to-all-start.5 = ((bf16[8,2,32768]{2,1,0:T(2,128)(2,1)}), bf16[8,2,32768]{2,1,0:T(2,128)(2,1)}, u32[]{:S(2)}, u32[]{:S(2)}) async-start(bf16[8,2,32768]{2,1,0:T(2,128)(2,1)} %reshape.519), calls=%async_computation.5 | async-start | bytes 2097152 | tf_op jit(solution)/shard_map/all_to_all | solution.py:391
  895.6 45.9 %all-to-all-start.7 = ((bf16[8,2,32768]{2,1,0:T(2,128)(2,1)}), bf16[8,2,32768]{2,1,0:T(2,128)(2,1)S(1)}, u32[]{:S(2)}, u32[]{:S(2)}) async-start(bf16[8,2,32768]{2,1,0:T(2,128)(2,1)} %reshape.515), calls=%async_computation.7 | async-start | bytes 2097152 | tf_op jit(solution)/shard_map/all_to_all | solution.py:397
  899.8 103.2 %reduce-scatter.11.cloned.1.call-start = ((), (), s32[]{:S(2)}) async-start(), calls=%async_computation.26 | async-start | bytes 1769472 | tf_op jit(solution)/shard_map/reduce_scatter | solution.py:435
  957.6 81.5 %reduce-scatter.9.cloned.1.call-start = ((), (), s32[]{:S(2)}) async-start(), calls=%async_computation.25 | async-start | bytes 1769472 | tf_op jit(solution)/shard_map/reduce_scatter | solution.py:432
  964.1 123.1 %reduce-scatter.19.cloned.1.call-start = ((), (), s32[]{:S(2)}) async-start(), calls=%async_computation.30 | async-start | bytes 3244032 | tf_op jit(solution)/shard_map/reduce_scatter | solution.py:447
  971.0 178.5 %all-reduce.9.cloned.1.call-start = ((), (), s32[]{:S(2)}) async-start(), calls=%async_computation.33 | async-start | bytes 2523136 | tf_op jit(solution)/shard_map/psum | solution.py:463
  989.0 98.3 %copy-start.78 = (f32[256]{0:T(256)S(1)}, f32[256]{0:T(256)}, u32[]{:S(2)}) copy-start(f32[256]{0:T(256)} %get-tuple-element.77) | copy-start | bytes 3076
  (80 other events, 1085.7 us)
Sparse Core Ops, SparseCore 0:
  9.9 29.5 all-gather.11
  41.3 125.2 all-gather.9
  168.5 25.7 all-gather.13
  196.1 146.4 all-gather.23
  344.3 65.6 all-gather.15
  411.8 26.3 all-gather.19
  440.0 213.9 all-gather.17
  656.5 31.0 all-gather.21
  689.5 25.0 all-gather.25
  758.6 34.2 reduce-scatter.14
  796.0 35.7 reduce-scatter.12
  834.7 36.9 reduce-scatter.22
  874.9 38.3 reduce-scatter.16
  916.5 39.3 reduce-scatter.20
  959.0 38.6 reduce-scatter.10
  1000.8 38.3 reduce-scatter.8
  1042.4 44.6 reduce-scatter.18
  1090.0 59.4 all-reduce.8
where the time goes:
time: 1170 us
  waiting for transfers between devices  537 us (46%)
  matrix products  277 us (24%)
  local copies, waits for them, and re-layouts  184 us (16%)
  blocking collectives  60 us (5%)
  other arithmetic  58.7 us (5%)
  starting transfers between devices  33.9 us (3%)
  between operations  15.8 us (1%)
    all_gather x1, waiting for transfers between devices, per_device(): gate_piece = lax.all_gather(gate_up_projection, 'shard', axis=0, tiled=True)  212 us
    all_gather x1, waiting for transfers between devices, per_device(): lax.all_gather(query_key_value_weight, 'shard', axis=0, tiled=True)  107 us
    psum x1, waiting for transfers between devices, per_device(): lax.psum(owner_sums[5].astype(jnp.bfloat16), 'rep').astype(jnp.float32)  57.2 us
    unnamed x183, local copies, waits for them, and re-layouts  51.7 us
    dot_general x8, matrix products, matrix_product_transposed_right(): lax.dot_general(factor, partner, (((1,), (1,)), ((), ())), preferred_elem...  50.5 us
    reduce_scatter x1, waiting for transfers between devices, per_device(): lax.psum_scatter(adapter_store.astype(jnp.bfloat16), 'shard', scatter_dim...  48 us
    dot_general x8, matrix products, matrix_product(): return jnp.dot(factor, partner, preferred_element_type=jnp.float32)  44.6 us
    reduce_scatter x1, waiting for transfers between devices, per_device(): lax.psum_scatter(qkv_a_grad.astype(jnp.bfloat16), 'shard', scatter_dimens...  36.2 us
  transfers between devices with their start and end apart: 26, of which 12 were waited for; matrix products, arithmetic and copies ran while one was open for 39% of the time, Pallas kernels for 0%

commit v1 on v0

v1 whole, which is shorter than its diff:
```python
import math

import jax
import jax.numpy as jnp
from jax import lax
from jax.sharding import PartitionSpec as P

HEAD_DIM = 64
ROT = 16
ADAPTER_COUNT = 8
RANK = 16
EXTRA = 128

adapter_scale = 2.0
norm_epsilon = 1e-05
rotary_base = 10000.0
masked_score = -1e30
low = jnp.bfloat16


def dot(a, b):
    return jnp.dot(a, b, preferred_element_type=jnp.float32)


def dot_nt(a, b):
    return lax.dot_general(a, b, (((1,), (1,)), ((), ())), preferred_element_type=jnp.float32)


def dot_tn(a, b):
    return lax.dot_general(a, b, (((0,), (0,)), ((), ())), preferred_element_type=jnp.float32)


def layer_norm(values, gain_row, shift_row):
    average = jnp.mean(values, axis=-1, keepdims=True)
    centered = values - average
    variance = jnp.mean(centered * centered, axis=-1, keepdims=True)
    inverse = lax.rsqrt(variance + norm_epsilon)
    unit_rows = centered * inverse
    return (unit_rows * gain_row + shift_row, unit_rows, inverse)


def layer_norm_back(grad_rows, unit_rows, inverse, gain_row):
    scaled = grad_rows * gain_row
    return inverse * (
        scaled
        - jnp.mean(scaled, axis=-1, keepdims=True)
        - unit_rows * jnp.mean(scaled * unit_rows, axis=-1, keepdims=True)
    )


def rotary_tables(span, heads_here):
    half_rot = ROT // 2
    lane = jnp.arange(heads_here * HEAD_DIM, dtype=jnp.int32) % HEAD_DIM
    turn = (lane % half_rot).astype(jnp.float32) * (-2.0 * math.log(rotary_base) / ROT)
    places = jnp.arange(span, dtype=jnp.int32).astype(jnp.float32)
    angles = places[:, None] * jnp.exp(turn)[None, :]
    cosine = jnp.where(lane[None, :] < ROT, jnp.cos(angles), 1.0)
    sine = jnp.sin(angles)
    sine_former = jnp.where(lane[None, :] < half_rot, -sine, 0.0)
    sine_latter = jnp.where((lane[None, :] >= half_rot) & (lane[None, :] < ROT), sine, 0.0)
    return (cosine, sine_former, sine_latter)


def turn_rows(values, tables):
    cosine, sine_former, sine_latter = tables
    half_rot = ROT // 2
    return (
        values * cosine
        + jnp.roll(values, -half_rot, axis=1) * sine_former
        + jnp.roll(values, half_rot, axis=1) * sine_latter
    )


def unturn_rows(grads, tables):
    cosine, sine_former, sine_latter = tables
    half_rot = ROT // 2
    return (
        grads * cosine
        + jnp.roll(grads * sine_former, half_rot, axis=1)
        + jnp.roll(grads * sine_latter, -half_rot, axis=1)
    )


def head_split(rows):
    return rows.reshape(rows.shape[0], -1, HEAD_DIM)


def attend(queries, keys, values, length):
    span = queries.shape[0]
    places = jnp.arange(span, dtype=jnp.int32)
    allowed = (places[None, :] <= places[:, None]) & (places[None, :] < length)
    scores = jnp.einsum(
        "qgd,kgd->gqk", head_split(queries), head_split(keys), preferred_element_type=jnp.float32
    ) * (HEAD_DIM**-0.5)
    scores = jnp.where(allowed[None], scores, masked_score)
    top = jnp.max(scores, axis=-1, keepdims=True)
    shifted = jnp.exp(scores - top)
    total = jnp.sum(shifted, axis=-1, keepdims=True)
    probabilities = shifted / total
    attended = jnp.einsum(
        "gqk,kgd->qgd",
        probabilities.astype(low),
        head_split(values),
        preferred_element_type=jnp.float32,
    )
    return (attended.reshape(span, -1), top + jnp.log(total))


def attend_back(queries, keys, values, lse, attended, grads, length):
    span = queries.shape[0]
    places = jnp.arange(span, dtype=jnp.int32)
    allowed = (places[None, :] <= places[:, None]) & (places[None, :] < length)
    q, k, v, g = (head_split(rows) for rows in (queries, keys, values, grads))
    delta = jnp.sum(g.astype(jnp.float32) * head_split(attended), axis=-1).T[:, :, None]
    scale = HEAD_DIM**-0.5
    scores = jnp.einsum("qgd,kgd->gqk", q, k, preferred_element_type=jnp.float32) * scale
    probabilities = jnp.where(allowed[None], jnp.exp(scores - lse), 0.0)
    prob_grad = jnp.einsum("qgd,kgd->gqk", g, v, preferred_element_type=jnp.float32)
    score_grad = (probabilities * (prob_grad - delta)).astype(low)
    q_grad = scale * jnp.einsum("gqk,kgd->qgd", score_grad, k, preferred_element_type=jnp.float32)
    k_grad = scale * jnp.einsum("gqk,qgd->kgd", score_grad, q, preferred_element_type=jnp.float32)
    v_grad = jnp.einsum(
        "gqk,qgd->kgd", probabilities.astype(low), g, preferred_element_type=jnp.float32
    )
    return tuple(rows.reshape(span, -1) for rows in (q_grad, k_grad, v_grad))


def pick_columns(table, adapter, blocks):
    width = ADAPTER_COUNT * RANK
    return jnp.concatenate(
        [
            lax.dynamic_slice_in_dim(table[:, j * width : (j + 1) * width], adapter * RANK, RANK, 1)
            for j in range(blocks)
        ],
        axis=1,
    )


def widen(*parts):
    rows = parts[0].shape[0]
    used = sum(part.shape[1] for part in parts[1:])
    return jnp.concatenate([*parts, jnp.zeros((rows, EXTRA - used), parts[0].dtype)], axis=1)


def gather_rows(rows):
    return lax.all_gather(rows, "shard", axis=0, tiled=True)


def scatter_rows(rows):
    return lax.psum_scatter(rows, "shard", scatter_dimension=0, tiled=True)


def per_device(
    tokens,
    lengths,
    slot_adapter_index,
    norm_gain_rows,
    norm_shift_rows,
    query_key_value_weight,
    query_key_value_bias,
    output_projection_weight,
    gate_up_projection,
    down_projection_weight,
    attention_adapter_input,
    attention_adapter_output,
    output_adapter_input,
    output_adapter_output,
    feedforward_adapter_input,
    feedforward_adapter_output,
    down_adapter_input,
    down_adapter_output,
    output_cotangent,
):
    slot_count, local_span, width = tokens.shape
    shards = lax.axis_size("shard")
    reps = lax.axis_size("rep")
    me = lax.axis_index("shard")
    span = local_span * shards
    own = width // shards
    hidden = gate_up_projection.shape[0]
    places = me * local_span + jnp.arange(local_span, dtype=jnp.int32)
    slots = range(slot_count)
    adapters = [slot_adapter_index[s] for s in slots]

    map_pieces = []
    for s in slots:
        a = adapters[s]
        rows_of = lambda table: lax.dynamic_slice_in_dim(table, a * RANK, RANK, 0).T
        map_pieces += [
            pick_columns(attention_adapter_input, a, 3),
            pick_columns(feedforward_adapter_input, a, 2),
            pick_columns(output_adapter_input, a, 1),
            rows_of(output_adapter_output),
            rows_of(down_adapter_output),
        ]
    maps = gather_rows(jnp.concatenate(map_pieces, axis=1)).reshape(width, slot_count, -1)

    weight_here = lax.all_to_all(
        query_key_value_weight.reshape(own, 3, shards, own), "shard", 2, 0, tiled=True
    ).reshape(width, 3 * own)
    bias_here = lax.dynamic_slice_in_dim(
        query_key_value_bias.reshape(3, width), me * own, own, 1
    ).reshape(1, 3 * own)
    output_full = gather_rows(output_projection_weight)
    tables = rotary_tables(span, own // HEAD_DIM)
    gate_up = gate_up_projection.reshape(hidden * 2, width)
    gate_weight = gate_up_projection[:, 0]
    up_weight = gate_up_projection[:, 1]

    kept = []
    for s in slots:
        a = adapters[s]
        own_maps = maps[:, s]
        qkv_in, mlp_in = (own_maps[:, :48], own_maps[:, 48:80])
        out_in, out_out, down_out = (own_maps[:, 80:96], own_maps[:, 96:112], own_maps[:, 112:128])
        valid = (places < lengths[s]).astype(jnp.float32)[:, None]
        inputs = tokens[s].astype(jnp.float32)
        grad_rows = output_cotangent[s].astype(jnp.float32) * valid
        grad_low = grad_rows.astype(low)
        down_mid_grad = (adapter_scale * dot(grad_low, down_out)).astype(low)
        normed, unit_one, inverse_one = layer_norm(inputs, norm_gain_rows[0], norm_shift_rows[0])
        normed = normed.astype(low)
        qkv_mid = dot(normed, qkv_in).astype(low)
        kept.append(
            dict(
                a=a,
                qkv_in=qkv_in,
                mlp_in=mlp_in,
                out_in=out_in,
                out_out=out_out,
                down_out=down_out,
                valid=valid,
                inputs=inputs,
                grad_rows=grad_rows,
                grad_low=grad_low,
                down_mid_grad=down_mid_grad,
                normed=normed,
                unit_one=unit_one,
                inverse_one=inverse_one,
                qkv_mid=qkv_mid,
                qkv_out=lax.dynamic_slice_in_dim(attention_adapter_output, a * RANK, RANK, 1),
                mlp_out=lax.dynamic_slice_in_dim(feedforward_adapter_output, a * RANK, RANK, 2),
                down_in=lax.dynamic_slice_in_dim(down_adapter_input, a * RANK, RANK, 1),
            )
        )

    for s in slots:
        k = kept[s]
        wide = gather_rows(widen(k["normed"], k["qkv_mid"]))
        k["all_mid"] = wide[:, width : width + 3 * RANK]
        projected = dot(wide[:, :width], weight_here) + bias_here
        update = jnp.concatenate(
            [
                dot(k["all_mid"][:, j * RANK : (j + 1) * RANK], k["qkv_out"][j])
                for j in range(3)
            ],
            axis=1,
        )
        projected = projected + adapter_scale * update
        k["q"] = turn_rows(projected[:, :own], tables).astype(low)
        k["k"] = turn_rows(projected[:, own : 2 * own], tables).astype(low)
        k["v"] = projected[:, 2 * own :].astype(low)
        k["attended"], k["lse"] = attend(k["q"], k["k"], k["v"], lengths[s])

    for s in slots:
        k = kept[s]
        attended = lax.all_to_all(k["attended"].astype(low), "shard", 0, 1, tiled=True)
        out_mid = dot(attended, k["out_in"]).astype(low)
        hidden_in = k["inputs"] + (
            dot(attended, output_full) + adapter_scale * dot_nt(out_mid, k["out_out"])
        )
        normed_two, unit_two, inverse_two = layer_norm(
            hidden_in, norm_gain_rows[1], norm_shift_rows[1]
        )
        normed_two = normed_two.astype(low)
        mlp_mid = dot(normed_two, k["mlp_in"]).astype(low)
        k.update(
            attended_rows=attended,
            out_mid=out_mid,
            hidden_in=hidden_in,
            normed_two=normed_two,
            unit_two=unit_two,
            inverse_two=inverse_two,
            mlp_mid=mlp_mid,
        )

    for s in slots:
        k = kept[s]
        wide = gather_rows(widen(k["normed_two"], k["mlp_mid"]))
        grad_wide = gather_rows(widen(k["grad_low"], k["down_mid_grad"]))
        two, mids = (wide[:, :width], wide[:, width : width + 2 * RANK])
        parts = []
        for j, weight in enumerate((gate_weight, up_weight)):
            mid = mids[:, j * RANK : (j + 1) * RANK]
            parts.append(
                dot_nt(two, weight) + adapter_scale * dot_nt(mid, k["mlp_out"][:, j])
            )
        gate, up = parts
        sigmoid = jax.nn.sigmoid(gate)
        silu = gate * sigmoid
        activated = (silu * up).astype(low)
        down_partial = jnp.concatenate(
            [
                dot(activated, down_projection_weight).astype(low),
                dot(activated, k["down_in"]).astype(low),
                jnp.zeros((span, EXTRA - RANK), low),
            ],
            axis=1,
        )
        down_mid_grad = grad_wide[:, width : width + RANK]
        hidden_grad = dot_nt(grad_wide[:, :width], down_projection_weight) + dot_nt(
            down_mid_grad, k["down_in"]
        )
        gate_grad = (hidden_grad * up * sigmoid * (1.0 + gate * (1.0 - sigmoid))).astype(low)
        up_grad = (hidden_grad * silu).astype(low)
        two_partial = jnp.concatenate(
            [
                (dot(gate_grad, gate_weight) + dot(up_grad, up_weight)).astype(low),
                (adapter_scale * dot(gate_grad, k["mlp_out"][:, 0])).astype(low),
                (adapter_scale * dot(up_grad, k["mlp_out"][:, 1])).astype(low),
                jnp.zeros((span, EXTRA - 2 * RANK), low),
            ],
            axis=1,
        )
        k["two_sum"] = scatter_rows(two_partial)
        k["down_sum"] = scatter_rows(down_partial)
        k["down_a"] = dot_tn(activated, down_mid_grad)
        k["mlp_b"] = adapter_scale * jnp.concatenate(
            [dot_tn(gate_grad, mids[:, :RANK]), dot_tn(up_grad, mids[:, RANK:])], axis=1
        )

    for s in slots:
        k = kept[s]
        mlp_mid_grad = k["two_sum"][:, width : width + 2 * RANK]
        two_grad = k["two_sum"][:, :width].astype(jnp.float32) + dot_nt(mlp_mid_grad, k["mlp_in"])
        residual_grad = k["grad_rows"] + layer_norm_back(
            two_grad, k["unit_two"], k["inverse_two"], norm_gain_rows[1]
        )
        branch = residual_grad.astype(low)
        out_mid_grad = (adapter_scale * dot(branch, k["out_out"])).astype(low)
        attended_grad = (dot_nt(branch, output_full) + dot_nt(out_mid_grad, k["out_in"])).astype(
            low
        )
        k.update(
            residual_grad=residual_grad,
            branch=branch,
            mlp_mid_grad=mlp_mid_grad,
            out_mid_grad=out_mid_grad,
        )
        k["head_grad"] = lax.all_to_all(attended_grad, "shard", 1, 0, tiled=True)

    for s in slots:
        k = kept[s]
        q_grad, k_grad, v_grad = attend_back(
            k["q"], k["k"], k["v"], k["lse"], k["attended"], k["head_grad"], lengths[s]
        )
        projected_grad = jnp.concatenate(
            [unturn_rows(q_grad, tables), unturn_rows(k_grad, tables), v_grad], axis=1
        ).astype(low)
        mid_parts = []
        b_parts = []
        for j in range(3):
            part = projected_grad[:, j * own : (j + 1) * own]
            mid_parts.append((adapter_scale * dot_nt(part, k["qkv_out"][j])).astype(low))
            b_parts.append(
                adapter_scale * dot_tn(k["all_mid"][:, j * RANK : (j + 1) * RANK], part)
            )
        k["qkv_b"] = jnp.stack(b_parts)
        k["one_sum"] = scatter_rows(
            jnp.concatenate(
                [
                    dot_nt(projected_grad, weight_here).astype(low),
                    *mid_parts,
                    jnp.zeros((span, EXTRA - 3 * RANK), low),
                ],
                axis=1,
            )
        )

    block_parts = []
    token_parts = []
    compact = []
    for s in slots:
        k = kept[s]
        down_mid = k["down_sum"][:, width : width + RANK]
        feed = k["down_sum"][:, :width].astype(jnp.float32) + adapter_scale * dot_nt(
            down_mid, k["down_out"]
        )
        block_parts.append(((k["hidden_in"] + feed) * k["valid"]).astype(low))
        mid_grad = k["one_sum"][:, width : width + 3 * RANK]
        normed_grad = k["one_sum"][:, :width].astype(jnp.float32) + dot_nt(mid_grad, k["qkv_in"])
        token_parts.append(
            k["residual_grad"]
            + layer_norm_back(normed_grad, k["unit_one"], k["inverse_one"], norm_gain_rows[0])
        )
        compact += [
            dot_tn(k["normed"], mid_grad),
            dot_tn(k["normed_two"], k["mlp_mid_grad"]),
            dot_tn(k["attended_rows"], k["out_mid_grad"]),
            adapter_scale * dot_tn(k["branch"], k["out_mid"]),
            adapter_scale * dot_tn(k["grad_low"], down_mid),
        ]
    owned = scatter_rows(jnp.concatenate(compact, axis=1).astype(low))

    owned = owned.reshape(own, slot_count, 8, RANK)
    grads = []
    for s in slots:
        k = kept[s]
        part = [owned[:, s, j] for j in range(8)]
        part += [k["qkv_b"][j].T.astype(low) for j in range(3)]
        part += [k["mlp_b"][:, :RANK].astype(low), k["mlp_b"][:, RANK:].astype(low)]
        part += [k["down_a"].astype(low)]
        grads.append(jnp.concatenate(part, axis=0))
    shared = lax.all_gather(jnp.stack(grads), "rep", axis=0, tiled=True)
    index = lax.all_gather(slot_adapter_index, "rep", axis=0, tiled=True)
    spread = (index[:, None] == jnp.arange(ADAPTER_COUNT, dtype=jnp.int32)[None, :]).astype(
        jnp.float32
    )
    full = jnp.einsum(
        "nxr,na->xar", shared.astype(jnp.float32), spread, precision=lax.Precision.HIGHEST
    ).reshape(shared.shape[1], ADAPTER_COUNT * RANK)
    pieces = [full[j * own : (j + 1) * own] for j in range(11)]
    rest = full[11 * own :].reshape(3, hidden, ADAPTER_COUNT * RANK)
    return (
        jnp.stack(block_parts),
        jnp.stack(token_parts),
        jnp.concatenate(pieces[:3], axis=1),
        jnp.stack([piece.T for piece in pieces[8:11]]),
        pieces[5],
        pieces[6].T,
        jnp.concatenate(pieces[3:5], axis=1),
        jnp.stack([rest[0], rest[1]], axis=1),
        rest[2],
        pieces[7].T,
    )


def solution(mesh):
    rows = P("shard", None)
    in_specs = (
        P("rep", "shard", None),
        P("rep"),
        P("rep"),
        P(),
        P(),
        rows,
        P(),
        rows,
        P("shard", None, None),
        rows,
        rows,
        P(None, None, "shard"),
        rows,
        P(None, "shard"),
        rows,
        P("shard", None, None),
        rows,
        P(None, "shard"),
        P("rep", "shard", None),
    )
    out_specs = (
        P("rep", "shard", None),
        P("rep", "shard", None),
        rows,
        P(None, None, "shard"),
        rows,
        P(None, "shard"),
        rows,
        P("shard", None, None),
        rows,
        P(None, "shard"),
    )
    return jax.shard_map(
        per_device, mesh=mesh, in_specs=in_specs, out_specs=out_specs, check_vma=False
    )
```

time: 1170 us -> 857 us (0.73)
  waiting for transfers between devices: 537 us -> 246 us
  blocking collectives: 60 us -> 9.03 us
  starting transfers between devices: 33.9 us -> 21.6 us
    all_gather x9, waiting for transfers between devices: 355 us -> 98.9 us  [the longest x8 72.3 us: gather_rows(): return lax.all_gather(rows, 'shard', axis=0, tiled=True)]
    all_gather x3 -> x0, blocking collectives: 60 us -> none  [the longest x1 34.4 us: per_device(): lax.all_gather(output_adapter_output, 'shard', axis=1, tiled=True)]
    psum x1 -> x0, waiting for transfers between devices: 57.2 us -> none  [per_device(): lax.psum(owner_sums[5].astype(jnp.bfloat16), 'rep').astype(jnp.float32)]
    concatenate x1 -> x15, local copies, waits for them, and re-layouts: 4.09 us -> 57.4 us  [the longest x2 15.8 us: per_device(): jnp.concatenate([dot_nt(projected_grad, weight_here).astype(low), *mid_pa...]
    slice x3 -> x46, local copies, waits for them, and re-layouts: 1.1 us -> 46.1 us  [the longest x1 12.9 us: per_device(): gate_weight = gate_up_projection[:, 0]]
    dot_general x2 -> x0, local copies, waits for them, and re-layouts: 32.7 us -> none  [matrix_product(): return jnp.dot(factor, partner, preferred_element_type=jnp.float32)]
    convert_element_type x13 -> x20, local copies, waits for them, and re-layouts: 41.9 us -> 9.97 us  [the longest x6 5.07 us: per_device(): (adapter_scale * dot_nt(part, k['qkv_out'][j])).astype(low)]
    all_to_all x8 -> x5, waiting for transfers between devices: 36.4 us -> 51.4 us  [the longest x1 38 us: per_device(): lax.all_to_all(query_key_value_weight.reshape(own, 3, shards, own), 'shar...]
  transfers between devices with their start and end apart: 26 -> 21, of which waited for: 12 -> 11; matrix products, arithmetic and copies ran while one was open for 39% -> 56% of each run, Pallas kernels for 0% -> 0%
where the time goes in v1:
time: 857 us; the launch traced here: 847 us
  matrix products  288 us (34%)
  waiting for transfers between devices  246 us (29%)
  local copies, waits for them, and re-layouts  194 us (23%)
  other arithmetic  70 us (8%)
  starting transfers between devices  21.6 us (3%)
  between operations  18.3 us (2%)
  blocking collectives  9.03 us (1%)
    dot_general x32, matrix products, dot_nt(): lax.dot_general(a, b, (((1,), (1,)), ((), ())), preferred_element_type=jn...  97.9 us
    reduce_scatter x7, waiting for transfers between devices, scatter_rows(): return lax.psum_scatter(rows, 'shard', scatter_dimension=0, tiled=True)  95.4 us
    dot_general x32, matrix products, dot(): return jnp.dot(a, b, preferred_element_type=jnp.float32)  82.2 us
    all_gather x8, waiting for transfers between devices, gather_rows(): return lax.all_gather(rows, 'shard', axis=0, tiled=True)  72.3 us
    unnamed x303, local copies, waits for them, and re-layouts  45.1 us
    dot_general x22, matrix products, dot_tn(): lax.dot_general(a, b, (((0,), (0,)), ((), ())), preferred_element_type=jn...  40.5 us
    all_to_all x1, waiting for transfers between devices, per_device(): lax.all_to_all(query_key_value_weight.reshape(own, 3, shards, own), 'shar...  38 us
    all_gather x1, waiting for transfers between devices, per_device(): shared = lax.all_gather(jnp.stack(grads), 'rep', axis=0, tiled=True)  26.6 us
  transfers between devices with their start and end apart: 21, of which 11 were waited for; matrix products, arithmetic and copies ran while one was open for 56% of the time, Pallas kernels for 0%

profile of v1, /device:TPU:0, one launch (start us, length us, event | category | flops | bytes accessed | tf_op | source)
XLA Modules:
  0.0 847.4 jit_solution(3561622926331899591)
XLA Ops:
  23.9 20.2 %all-gather.10.cloned.1.call-done = bf16[2048,256]{0,1:T(8,128)(2,1)} async-done(((bf16[256,256]{0,1:T(8,128)(2,1)}), bf16[2048,256]{0,1:T(8,128)(2,1)}) %all-gather.10.cloned.1.call-update) | async-done | bytes 1048592 | tf_op jit(solution)/shard_map/all_gather | solution.py:146
  78.5 38.0 %all-to-all-done = bf16[256,3,8,256]{0,3,1,2:T(8,128)(2,1)} async-done(((bf16[256,3,8,256]{0,3,1,2:T(8,128)(2,1)}), bf16[256,3,8,256]{0,3,1,2:T(8,128)(2,1)}, u32[]{:S(2)}, u32[]{:S(2)}) %all-to-all-start) | async-done | bytes 3145760 | tf_op jit(solution)/shard_map/all_to_all | solution.py:198
  136.0 16.6 %all-gather.18.cloned.1.call-done = bf16[1024,2176]{1,0:T(8,128)(2,1)} async-done(((bf16[128,2176]{1,0:T(8,128)(2,1)}), bf16[1024,2176]{1,0:T(8,128)(2,1)}) %all-gather.18.cloned.1.call-update) | async-done | bytes 4456464 | tf_op jit(solution)/shard_map/all_gather | solution.py:146
  190.8 8.2 fusion.152
  220.5 11.3 %all-to-all-done.1 = bf16[8,128,256]{1,2,0:T(8,128)(2,1)} async-done(((bf16[8,128,256]{1,2,0:T(8,128)(2,1)}), bf16[8,128,256]{1,2,0:T(8,128)(2,1)}, u32[]{:S(2)}, u32[]{:S(2)}) %all-to-all-start.1) | async-done | bytes 524320 | tf_op jit(solution)/shard_map/all_to_all | solution.py:267
  255.4 12.9 %fusion.307 = (bf16[704,1,2048]{2,1,0:T(2,128)(2,1)}, bf16[704,1,2048]{2,1,0:T(2,128)(2,1)}) fusion(bf16[704,2,2048]{2,1,0:T(2,128)(2,1)} %param.27), kind=kLoop, calls=%fused_computation.504 | loop fusion | bytes 11534336 | tf_op jit(solution)/shard_map/slice | solution.py:207
  273.5 10.5 %copy_bitcast_fusion = (bf16[704,2048]{1,0:T(8,128)(2,1)}, bf16[704,2048]{1,0:T(8,128)(2,1)}) fusion(bf16[704,1,2048]{2,1,0:T(2,128)(2,1)} %get-tuple-element.69, bf16[704,1,2048]{2,1,0:T(2,128)(2,1)} %get-tuple-element.68), kind=kLoop, calls=%fused_computation.50 | loop fusion | bytes 11534336 | tf_op jit(solution)/shard_map/squeeze | solution.py:208
  284.0 7.0 fusion.14
  327.5 7.8 concatenate.143
  336.7 6.9 fusion.12
  343.6 31.6 %all-gather.20.cloned.1.call-done = bf16[1024,2176]{1,0:T(8,128)(2,1)} async-done(((bf16[128,2176]{1,0:T(8,128)(2,1)}), bf16[1024,2176]{1,0:T(8,128)(2,1)}) %all-gather.20.cloned.1.call-update) | async-done | bytes 4456464 | tf_op jit(solution)/shard_map/all_gather | solution.py:146
  375.3 6.4 fusion.22
  408.4 7.8 concatenate.151
  419.1 6.6 convolution_convert_fusion
  425.7 7.8 concatenate.141
  442.8 8.0 concatenate.133
  454.4 32.8 %reduce-scatter.16.cloned.1.call-done = bf16[128,2176]{1,0:T(8,128)(2,1)} async-done(((bf16[1024,2176]{1,0:T(8,128)(2,1)}), bf16[128,2176]{1,0:T(8,128)(2,1)}) %reduce-scatter.16.cloned.1.call-update) | async-done | bytes 557072 | tf_op jit(solution)/shard_map/reduce_scatter | solution.py:150
  494.1 6.7 fusion.294
  509.1 6.7 fusion.290
  531.1 9.7 %multiply_convert_fusion.1 = bf16[4,1024,1024]{1,2,0:T(8,128)(2,1)S(1)} fusion(f32[4,1024,1024]{1,2,0:T(8,128)} %copy-done.3, bf16[1024,4,64]{0,2,1:T(8,128)(2,1)S(1)} %reshape.364, bf16[1024,4,64]{0,2,1:T(8,128)(2,1)} %bitcast.425, f32[4,1024]{1,0:T(4,128)S(1)} %bitcast.449, f32[4,1024]{1,0:T(4,128)S(1)} %log_add_fusion.1, pred[1024,1024]{0,1:T(8,128)(4,1)} %fusion.21), kind=kOutput, calls=%fused_computation.2 | convolution fusion | flops 562036736 | bytes 27295744 | tf_op jit(solution)/shard_map/qgd,kgd->gqk/dot_general | solution.py:118
  552.1 10.2 %multiply_convert_fusion = bf16[4,1024,1024]{1,2,0:T(8,128)(2,1)S(1)} fusion(f32[4,1024,1024]{1,2,0:T(8,128)} %copy-done.2, bf16[1024,4,64]{0,2,1:T(8,128)(2,1)S(1)} %reshape.368, bf16[1024,4,64]{0,2,1:T(8,128)(2,1)} %bitcast.424, f32[4,1024]{1,0:T(4,128)S(1)} %bitcast.450, f32[4,1024]{1,0:T(4,128)S(1)} %log_add_fusion, pred[1024,1024]{0,1:T(8,128)(4,1)} %fusion.20), kind=kOutput, calls=%fused_computation | convolution fusion | flops 562036736 | bytes 27295744 | tf_op jit(solution)/shard_map/qgd,kgd->gqk/dot_general | solution.py:118
  580.1 7.8 fusion.96
  590.4 7.5 fusion.181
  607.7 7.8 convolution_convert_fusion.3
  616.2 7.9 concatenate.149
  624.2 9.8 %fusion.99 = bf16[4,64,1024]{2,1,0:T(8,128)(2,1)S(1)} fusion(bf16[1024,4,64]{0,2,1:T(8,128)(2,1)} %copy-done.54, f32[4,1024,1024]{1,2,0:T(8,128)} %copy-done.2, f32[4,1024]{1,0:T(4,128)S(1)} %log_add_fusion, pred[1024,1024]{0,1:T(8,128)(4,1)} %fusion.20), kind=kOutput, calls=%fused_computation.158 | convolution fusion | flops 553910272 | bytes 18890752 | tf_op jit(solution)/shard_map/gqk,qgd->kgd/dot_general | solution.py:122
  640.3 7.8 convolution_convert_fusion.2
  648.1 7.9 concatenate.157
  658.2 9.0 %all-reduce = s32[8]{0:T(128)} all-reduce(s32[8]{0:T(128)S(1)} %dynamic-update-slice), channel_id=1, replica_groups=mesh['shard'=8,'rep'=4] {'rep'}, use_global_device_ids=true, to_apply=%add | all-reduce | flops 8 | bytes 64
  694.4 39.6 %reduce-scatter.18.cloned.1.call-done = bf16[128,2176]{1,0:T(8,128)(2,1)} async-done(((bf16[1024,2176]{1,0:T(8,128)(2,1)}), bf16[128,2176]{1,0:T(8,128)(2,1)}) %reduce-scatter.18.cloned.1.call-update) | async-done | bytes 557072 | tf_op jit(solution)/shard_map/reduce_scatter | solution.py:150
  756.6 23.0 %reduce-scatter.20.cloned.1.call-done = bf16[256,256]{0,1:T(8,128)(2,1)} async-done(((bf16[2048,256]{0,1:T(8,128)(2,1)}), bf16[256,256]{0,1:T(8,128)(2,1)}) %reduce-scatter.20.cloned.1.call-update) | async-done | bytes 131088 | tf_op jit(solution)/shard_map/reduce_scatter | solution.py:150
  787.6 26.6 %all-gather.26.cloned.1.call-done = bf16[8,4928,16]{1,2,0:T(8,128)(2,1)} async-done(((bf16[2,4928,16]{1,2,0:T(8,128)(2,1)}), bf16[8,4928,16]{1,2,0:T(8,128)(2,1)}) %all-gather.26.cloned.1.call-update) | async-done | bytes 1261584 | tf_op jit(solution)/shard_map/all_gather | solution.py:414
  (588 shorter events, 401.0 us)
Async XLA Ops:
  7.2 276.9 %copy-start = (bf16[704,2048]{1,0:T(8,128)(2,1)S(1)}, bf16[704,2048]{1,0:T(8,128)(2,1)}, u32[]{:S(2)}) copy-start(bf16[704,2048]{1,0:T(8,128)(2,1)} %param.28) | copy-start | bytes 8650756
  7.2 36.9 %all-gather.10.cloned.1.call-start = ((), (), s32[]{:S(2)}) async-start(), calls=%async_computation.12 | async-start | bytes 1179648 | tf_op jit(solution)/shard_map/all_gather | solution.py:146
  17.7 105.3 %all-gather.12.cloned.1.call-start = ((), (), s32[]{:S(2)}) async-start(), calls=%async_computation.13 | async-start | bytes 5013504 | tf_op jit(solution)/shard_map/all_gather | solution.py:146
  20.9 223.1 %copy-start.75 = (f32[1,2048]{1,0:T(1,128)}, f32[1,2048]{1,0:T(1,128)S(1)}, u32[]{:S(2)}) copy-start(f32[1,2048]{1,0:T(1,128)S(1)} %get-tuple-element.165) | copy-start | bytes 24580
  50.4 102.2 %all-gather.18.cloned.1.call-start = ((), (), s32[]{:S(2)}) async-start(), calls=%async_computation.17 | async-start | bytes 5013504 | tf_op jit(solution)/shard_map/all_gather | solution.py:146
  52.7 180.3 %all-gather.14.cloned.1.call-start = ((), (), s32[]{:S(2)}) async-start(), calls=%async_computation.14 | async-start | bytes 9437184 | tf_op jit(solution)/shard_map/all_gather | solution.py:146
  62.1 54.4 %all-to-all-start = ((bf16[256,3,8,256]{0,3,1,2:T(8,128)(2,1)}), bf16[256,3,8,256]{0,3,1,2:T(8,128)(2,1)}, u32[]{:S(2)}, u32[]{:S(2)}) async-start(bf16[256,3,8,256]{0,3,1,2:T(8,128)(2,1)} %copy.282), calls=%async_computation | async-start | bytes 6291456 | tf_op jit(solution)/shard_map/all_to_all | solution.py:198
  66.7 217.3 %all-gather.22.cloned.1.call-start = ((), (), s32[]{:S(2)}) async-start(), calls=%async_computation.20 | async-start | bytes 5013504 | tf_op jit(solution)/shard_map/all_gather | solution.py:146
  66.8 60.3 %copy-start.118 = (f32[768]{0:T(1024)}, f32[768]{0:T(1024)S(1)}, u32[]{:S(2)}) copy-start(f32[768]{0:T(1024)S(1)} %add.422) | copy-start | bytes 9220
  67.4 123.4 %copy-start.90 = (f32[256]{0:T(256)}, f32[256]{0:T(256)S(1)}, u32[]{:S(2)}) copy-start(f32[256]{0:T(256)S(1)} %fusion.284) | copy-start | bytes 3076
  71.3 119.5 %copy-start.69 = (f32[1024]{0:T(1024)}, f32[1024]{0:T(1024)S(1)}, u32[]{:S(2)}) copy-start(f32[1024]{0:T(1024)S(1)} %iota_convert_fusion) | copy-start | bytes 12292
  76.1 44.1 %copy-start.25 = (bf16[128,2048]{1,0:T(8,128)(2,1)}, bf16[128,2048]{1,0:T(8,128)(2,1)S(1)}, u32[]{:S(2)}) copy-start(bf16[128,2048]{1,0:T(8,128)(2,1)S(1)} %get-tuple-element.118) | copy-start | bytes 1572868
  187.3 28.0 %all-to-all-start.2 = ((bf16[8,128,256]{1,2,0:T(8,128)(2,1)}), bf16[8,128,256]{1,2,0:T(8,128)(2,1)S(1)}, u32[]{:S(2)}, u32[]{:S(2)}) async-start(bf16[8,128,256]{1,2,0:T(8,128)(2,1)} %copy.293), calls=%async_computation.3 | async-start | bytes 1048576 | tf_op jit(solution)/shard_map/all_to_all | solution.py:267
  215.3 16.5 %all-to-all-start.1 = ((bf16[8,128,256]{1,2,0:T(8,128)(2,1)}), bf16[8,128,256]{1,2,0:T(8,128)(2,1)}, u32[]{:S(2)}, u32[]{:S(2)}) async-start(bf16[8,128,256]{1,2,0:T(8,128)(2,1)} %copy.285), calls=%async_computation.1 | async-start | bytes 1048576 | tf_op jit(solution)/shard_map/all_to_all | solution.py:267
  219.4 75.5 %all-gather.16.cloned.1.call-start = ((), (), s32[]{:S(2)}) async-start(), calls=%async_computation.15 | async-start | bytes 5013504 | tf_op jit(solution)/shard_map/all_gather | solution.py:146
  249.3 87.4 %all-gather.24.cloned.1.call-start = ((), (), s32[]{:S(2)}) async-start(), calls=%async_computation.23 | async-start | bytes 5013504 | tf_op jit(solution)/shard_map/all_gather | solution.py:146
  251.5 123.7 %all-gather.20.cloned.1.call-start = ((), (), s32[]{:S(2)}) async-start(), calls=%async_computation.18 | async-start | bytes 5013504 | tf_op jit(solution)/shard_map/all_gather | solution.py:146
  255.4 195.5 %reduce-scatter.12.cloned.1.call-start = ((), (), s32[]{:S(2)}) async-start(), calls=%async_computation.21 | async-start | bytes 5013504 | tf_op jit(solution)/shard_map/reduce_scatter | solution.py:150
  335.4 151.8 %reduce-scatter.16.cloned.1.call-start = ((), (), s32[]{:S(2)}) async-start(), calls=%async_computation.24 | async-start | bytes 5013504 | tf_op jit(solution)/shard_map/reduce_scatter | solution.py:150
  416.2 261.5 %reduce-scatter.10.cloned.1.call-start = ((), (), s32[]{:S(2)}) async-start(), calls=%async_computation.19 | async-start | bytes 5013504 | tf_op jit(solution)/shard_map/reduce_scatter | solution.py:150
  433.5 246.8 %reduce-scatter.8.cloned.1.call-start = ((), (), s32[]{:S(2)}) async-start(), calls=%async_computation.16 | async-start | bytes 5013504 | tf_op jit(solution)/shard_map/reduce_scatter | solution.py:150
  450.8 36.3 %copy-start.45 = (bf16[2048,128]{0,1:T(8,128)(2,1)S(1)}, bf16[2048,128]{0,1:T(8,128)(2,1)}, u32[]{:S(2)}) copy-start(bf16[2048,128]{0,1:T(8,128)(2,1)} %get-tuple-element.121) | copy-start | bytes 1572868
  450.8 36.3 %copy-start.107 = (f32[128]{0:T(128)S(1)}, f32[128]{0:T(128)}, u32[]{:S(2)}) copy-start(f32[128]{0:T(128)} %copy-done.106) | copy-start | bytes 1540
  450.9 38.2 %copy-start.102 = (f32[128]{0:T(128)S(1)}, f32[128]{0:T(128)}, u32[]{:S(2)}) copy-start(f32[128]{0:T(128)} %copy-done.101) | copy-start | bytes 1540
  450.9 38.2 %copy-start.104 = (f32[128]{0:T(128)S(1)}, f32[128]{0:T(128)}, u32[]{:S(2)}) copy-start(f32[128]{0:T(128)} %copy-done.103) | copy-start | bytes 1540
  504.9 17.0 %all-to-all-start.3 = ((bf16[128,8,256]{0,2,1:T(8,128)(2,1)}), bf16[128,8,256]{0,2,1:T(8,128)(2,1)}, u32[]{:S(2)}, u32[]{:S(2)}) async-start(bf16[128,8,256]{0,2,1:T(8,128)(2,1)} %bitcast.414), calls=%async_computation.6 | async-start | bytes 1048576 | tf_op jit(solution)/shard_map/all_to_all | solution.py:350
  521.9 25.2 %all-to-all-start.4 = ((bf16[128,8,256]{0,2,1:T(8,128)(2,1)}), bf16[128,8,256]{0,2,1:T(8,128)(2,1)}, u32[]{:S(2)}, u32[]{:S(2)}) async-start(bf16[128,8,256]{0,2,1:T(8,128)(2,1)} %bitcast.63), calls=%async_computation.9 | async-start | bytes 1048576 | tf_op jit(solution)/shard_map/all_to_all | solution.py:350
  526.1 158.2 %reduce-scatter.14.cloned.1.call-start = ((), (), s32[]{:S(2)}) async-start(), calls=%async_computation.22 | async-start | bytes 5013504 | tf_op jit(solution)/shard_map/reduce_scatter | solution.py:150
  624.1 109.8 %reduce-scatter.18.cloned.1.call-start = ((), (), s32[]{:S(2)}) async-start(), calls=%async_computation.25 | async-start | bytes 5013504 | tf_op jit(solution)/shard_map/reduce_scatter | solution.py:150
  656.1 123.5 %reduce-scatter.20.cloned.1.call-start = ((), (), s32[]{:S(2)}) async-start(), calls=%async_computation.26 | async-start | bytes 1179648 | tf_op jit(solution)/shard_map/reduce_scatter | solution.py:150
  680.3 57.6 %copy-start.18 = (bf16[8,128,256]{1,2,0:T(8,128)(2,1)S(1)}, bf16[8,128,256]{1,2,0:T(8,128)(2,1)}, u32[]{:S(2)}) copy-start(bf16[8,128,256]{1,2,0:T(8,128)(2,1)} %copy-done.17) | copy-start | bytes 1572868
  743.4 70.8 %all-gather.26.cloned.1.call-start = ((), (), s32[]{:S(2)}) async-start(), calls=%async_computation.27 | async-start | bytes 1597440 | tf_op jit(solution)/shard_map/all_gather | solution.py:414
  (119 other events, 960.3 us)
Sparse Core Ops, SparseCore 0:
  17.8 26.1 all-gather.9
  50.5 57.8 all-gather.11
  110.9 41.6 all-gather.17
  154.3 59.8 all-gather.13
  216.0 39.4 all-gather.21
  257.2 37.6 all-gather.15
  297.4 37.6 all-gather.23
  337.5 37.6 all-gather.19
  378.7 52.5 reduce-scatter.11
  434.6 52.5 reduce-scatter.15
  490.6 56.8 reduce-scatter.9
  550.8 52.5 reduce-scatter.7
  624.2 53.7 reduce-scatter.13
  681.4 52.5 reduce-scatter.17
  743.6 35.9 reduce-scatter.19
  782.3 31.9 all-gather.25

commit v2 on v1

v2 whole, which is shorter than its diff:
```python
import math

import jax
import jax.numpy as jnp
from jax import lax
from jax.experimental import pallas as pl
from jax.experimental.pallas import tpu as pltpu
from jax.sharding import PartitionSpec as P

HEAD_DIM = 64
ROT = 16
ADAPTER_COUNT = 8
RANK = 16
EXTRA = 128

adapter_scale = 2.0
norm_epsilon = 1e-05
rotary_base = 10000.0
masked_score = -1e30
low = jnp.bfloat16


def dot(a, b):
    return jnp.dot(a, b, preferred_element_type=jnp.float32)


def dot_nt(a, b):
    return lax.dot_general(a, b, (((1,), (1,)), ((), ())), preferred_element_type=jnp.float32)


def dot_tn(a, b):
    return lax.dot_general(a, b, (((0,), (0,)), ((), ())), preferred_element_type=jnp.float32)


def layer_norm(values, gain_row, shift_row):
    average = jnp.mean(values, axis=-1, keepdims=True)
    centered = values - average
    variance = jnp.mean(centered * centered, axis=-1, keepdims=True)
    inverse = lax.rsqrt(variance + norm_epsilon)
    unit_rows = centered * inverse
    return (unit_rows * gain_row + shift_row, unit_rows, inverse)


def layer_norm_back(grad_rows, unit_rows, inverse, gain_row):
    scaled = grad_rows * gain_row
    return inverse * (
        scaled
        - jnp.mean(scaled, axis=-1, keepdims=True)
        - unit_rows * jnp.mean(scaled * unit_rows, axis=-1, keepdims=True)
    )


def rotary_tables(span, heads_here):
    half_rot = ROT // 2
    lane = jnp.arange(heads_here * HEAD_DIM, dtype=jnp.int32) % HEAD_DIM
    turn = (lane % half_rot).astype(jnp.float32) * (-2.0 * math.log(rotary_base) / ROT)
    places = jnp.arange(span, dtype=jnp.int32).astype(jnp.float32)
    angles = places[:, None] * jnp.exp(turn)[None, :]
    cosine = jnp.where(lane[None, :] < ROT, jnp.cos(angles), 1.0)
    sine = jnp.sin(angles)
    sine_former = jnp.where(lane[None, :] < half_rot, -sine, 0.0)
    sine_latter = jnp.where((lane[None, :] >= half_rot) & (lane[None, :] < ROT), sine, 0.0)
    return (cosine, sine_former, sine_latter)


def turn_rows(values, tables):
    cosine, sine_former, sine_latter = tables
    half_rot = ROT // 2
    lanes = values.shape[1]
    return (
        values * cosine
        + pltpu.roll(values, lanes - half_rot, 1) * sine_former
        + pltpu.roll(values, half_rot, 1) * sine_latter
    )


def unturn_rows(grads, tables):
    cosine, sine_former, sine_latter = tables
    half_rot = ROT // 2
    lanes = grads.shape[1]
    return (
        grads * cosine
        + pltpu.roll(grads * sine_former, half_rot, 1)
        + pltpu.roll(grads * sine_latter, lanes - half_rot, 1)
    )


def whole(shape):
    return pl.BlockSpec(shape, lambda i, *_: (0,) * len(shape), pipeline_mode=pl.Buffered(1))


def kept_out(shape):
    return pl.BlockSpec(shape, lambda i, *_: (0,) * len(shape))


def allowed_keys(first_row, rows, keys, length):
    query = first_row + lax.broadcasted_iota(jnp.int32, (rows, keys), 0)
    key = lax.broadcasted_iota(jnp.int32, (rows, keys), 1)
    return (key <= query) & (key < length)


def attend_kernel(
    lengths_ref, wide_ref, weight_ref, maps_ref, bias_ref, cos_ref, sf_ref, sl_ref,
    q_ref, k_ref, v_ref, low_ref, att_ref, lse_ref, *, slot, steps
):
    rows = wide_ref.shape[0]
    own = q_ref.shape[1]
    width = weight_ref.shape[0]
    step = pl.program_id(0)
    length = lengths_ref[slot]
    heads = own // HEAD_DIM
    tables = (cos_ref[...], sf_ref[...], sl_ref[...])
    projected = (
        dot(wide_ref[:, :width], weight_ref[...])
        + bias_ref[...]
        + dot(wide_ref[:, width:], maps_ref[...])
    )
    head_lane = lax.broadcasted_iota(jnp.int32, (rows, own), 1) // HEAD_DIM
    lse_lane = lax.broadcasted_iota(jnp.int32, (rows, 128), 1)
    here = pl.ds(pl.multiple_of(step * rows, rows), rows)
    queries = (turn_rows(projected[:, :own], tables).astype(low)) * low(HEAD_DIM**-0.5)
    q_ref[here, :] = queries
    k_ref[here, :] = turn_rows(projected[:, own : 2 * own], tables).astype(low)
    v_ref[here, :] = projected[:, 2 * own :].astype(low)
    for i in range(steps):

        @pl.when(step == i)
        def _():
            span = (i + 1) * rows
            keys = k_ref[:span, :]
            values = v_ref[:span, :]
            allowed = allowed_keys(i * rows, rows, span, length)
            attended = jnp.zeros((rows, own), jnp.float32)
            lse = jnp.zeros((rows, 128), jnp.float32)
            for h in range(heads):
                scores = dot_nt(jnp.where(head_lane == h, queries, low(0)), keys)
                scores = jnp.where(allowed, scores, masked_score)
                top = jnp.max(scores, axis=1, keepdims=True)
                shifted = jnp.exp(scores - top)
                total = jnp.sum(shifted, axis=1, keepdims=True)
                probabilities = (shifted * (1.0 / total)).astype(low)
                attended = jnp.where(head_lane == h, dot(probabilities, values), attended)
                lse = jnp.where(lse_lane == h, top + jnp.log(total), lse)
            att_ref[...] = attended
            low_ref[...] = attended.astype(low)
            lse_ref[...] = lse


def attend(lengths, wide, weight, maps, bias, tables, slot):
    span, columns = wide.shape
    width, three_own = weight.shape
    own = three_own // 3
    rows = 256
    block = lambda n: pl.BlockSpec((rows, n), lambda i, *_: (i, 0))
    return pl.pallas_call(
        lambda *refs: attend_kernel(*refs, slot=slot, steps=span // rows),
        grid_spec=pltpu.PrefetchScalarGridSpec(
            num_scalar_prefetch=1,
            grid=(span // rows,),
            in_specs=[
                block(columns),
                whole(weight.shape),
                whole(maps.shape),
                whole(bias.shape),
                block(own),
                block(own),
                block(own),
            ],
            out_specs=[
                kept_out((span, own)),
                kept_out((span, own)),
                kept_out((span, own)),
                block(own),
                block(own),
                block(128),
            ],
        ),
        out_shape=[
            jax.ShapeDtypeStruct((span, own), low),
            jax.ShapeDtypeStruct((span, own), low),
            jax.ShapeDtypeStruct((span, own), low),
            jax.ShapeDtypeStruct((span, own), low),
            jax.ShapeDtypeStruct((span, own), jnp.float32),
            jax.ShapeDtypeStruct((span, 128), jnp.float32),
        ],
        compiler_params=pltpu.CompilerParams(vmem_limit_bytes=56 << 20),
        cost_estimate=pl.CostEstimate(
            flops=2 * span * columns * three_own + 16 * span * span * 64 * own // HEAD_DIM,
            bytes_accessed=2 * (span * columns + width * three_own),
            transcendentals=span * span,
        ),
        name="attend",
    )(lengths, wide, weight, maps, bias, *tables)


def attend_back_kernel(
    lengths_ref, q_ref, k_ref, v_ref, lse_ref, att_ref, g_ref, mid_ref, weight_ref, maps_ref,
    cos_ref, sf_ref, sl_ref, out_ref, b_ref, dq_ref, dk_ref, dv_ref, *, slot, steps
):
    rows = out_ref.shape[0]
    own = q_ref.shape[1]
    width = weight_ref.shape[0]
    heads = own // HEAD_DIM
    step = pl.program_id(0)
    length = lengths_ref[slot]
    head_lane = lax.broadcasted_iota(jnp.int32, (rows, own), 1) // HEAD_DIM

    @pl.when(step == 0)
    def _():
        dk_ref[...] = jnp.zeros_like(dk_ref)
        dv_ref[...] = jnp.zeros_like(dv_ref)
        b_ref[...] = jnp.zeros_like(b_ref)

    for i in range(steps):

        @pl.when(step == i)
        def _():
            span = (i + 1) * rows
            mine = slice(i * rows, (i + 1) * rows)
            queries, grads = (q_ref[mine, :], g_ref[mine, :])
            keys, values = (k_ref[:span, :], v_ref[:span, :])
            products = grads.astype(jnp.float32) * att_ref[mine, :]
            allowed = allowed_keys(i * rows, rows, span, length)
            dq = jnp.zeros((rows, own), jnp.float32)
            for h in range(heads):
                mask = head_lane == h
                query = jnp.where(mask, queries, low(0))
                grad = jnp.where(mask, grads, low(0))
                delta = jnp.sum(jnp.where(mask, products, 0.0), axis=1, keepdims=True)
                scores = dot_nt(query, keys)
                probabilities = jnp.where(
                    allowed, jnp.exp(scores - lse_ref[mine, h : h + 1]), 0.0
                )
                score_grad = (probabilities * (dot_nt(grad, values) - delta)).astype(low)
                dq = jnp.where(mask, dot(score_grad, keys), dq)
                dk_ref[:span, :] += dot_tn(score_grad, query)
                dv_ref[:span, :] += dot_tn(probabilities.astype(low), grad)
            dq_ref[mine, :] = dq * (HEAD_DIM**-0.5)

    @pl.when(step >= steps)
    def _():
        here = pl.ds(pl.multiple_of((step - steps) * rows, rows), rows)
        tables = (cos_ref[...], sf_ref[...], sl_ref[...])
        parts = (
            unturn_rows(dq_ref[here, :], tables).astype(low),
            unturn_rows(dk_ref[here, :], tables).astype(low),
            dv_ref[here, :].astype(low),
        )
        total = jnp.zeros((rows, width), jnp.float32)
        extra = jnp.zeros((rows, EXTRA), jnp.float32)
        for j, part in enumerate(parts):
            columns = slice(j * own, (j + 1) * own)
            total += dot_nt(part, weight_ref[:, columns])
            extra += dot_nt(part, maps_ref[:, columns])
            b_ref[:, columns] += adapter_scale * dot_tn(mid_ref[...], part)
        out_ref[:, :width] = total.astype(low)
        out_ref[:, width:] = extra.astype(low)


def attend_back(lengths, q, k, v, lse, att, grads, wide, weight, maps, tables, slot):
    span, own = q.shape
    width = weight.shape[0]
    rows = 256
    steps = span // rows
    late = lambda i: jnp.maximum(i - steps, 0)
    block = lambda n: pl.BlockSpec((rows, n), lambda i, *_: (late(i), 0))
    return pl.pallas_call(
        lambda *refs: attend_back_kernel(*refs, slot=slot, steps=steps),
        grid_spec=pltpu.PrefetchScalarGridSpec(
            num_scalar_prefetch=1,
            grid=(2 * steps,),
            in_specs=[
                whole(q.shape),
                whole(q.shape),
                whole(q.shape),
                whole(lse.shape),
                whole(att.shape),
                whole(grads.shape),
                pl.BlockSpec((rows, EXTRA), lambda i, *_: (late(i), width // EXTRA)),
                whole(weight.shape),
                whole(maps.shape),
                block(own),
                block(own),
                block(own),
            ],
            out_specs=[block(width + EXTRA), kept_out((EXTRA, 3 * own))],
            scratch_shapes=[pltpu.VMEM((span, own), jnp.float32)] * 3,
        ),
        out_shape=[
            jax.ShapeDtypeStruct((span, width + EXTRA), low),
            jax.ShapeDtypeStruct((EXTRA, 3 * own), jnp.float32),
        ],
        compiler_params=pltpu.CompilerParams(vmem_limit_bytes=56 << 20),
        cost_estimate=pl.CostEstimate(
            flops=2 * span * width * 3 * own + 40 * span * span * 64 * own // HEAD_DIM,
            bytes_accessed=2 * (span * width + width * 3 * own),
            transcendentals=span * span,
        ),
        name="attend_back",
    )(lengths, q, k, v, lse, att, grads, wide, weight, maps, *tables)


def mlp_kernel(
    wide_ref, grad_ref, gu_ref, down_ref, gate_map_ref, up_map_ref, down_map_ref,
    down_out_ref, two_out_ref, g_gate_ref, g_up_ref, g_down_ref
):
    width = down_ref.shape[1]

    @pl.when(pl.program_id(0) == 0)
    def _():
        g_gate_ref[...] = jnp.zeros_like(g_gate_ref)
        g_up_ref[...] = jnp.zeros_like(g_up_ref)
        g_down_ref[...] = jnp.zeros_like(g_down_ref)

    two, mids = (wide_ref[:, :width], wide_ref[:, width:])
    grad_mid = grad_ref[:, width:]
    gate = dot_nt(two, gu_ref[:, :width]) + dot_nt(mids, gate_map_ref[...])
    up = dot_nt(two, gu_ref[:, width:]) + dot_nt(mids, up_map_ref[...])
    hidden_grad = dot_nt(grad_ref[:, :width], down_ref[...]) + dot_nt(grad_mid, down_map_ref[...])
    sigmoid = 1.0 / (1.0 + jnp.exp(-gate))
    silu = gate * sigmoid
    activated = (silu * up).astype(low)
    gate_grad = (hidden_grad * up * sigmoid * (1.0 + gate * (1.0 - sigmoid))).astype(low)
    up_grad = (hidden_grad * silu).astype(low)
    two_out_ref[:, :width] = (
        dot(gate_grad, gu_ref[:, :width]) + dot(up_grad, gu_ref[:, width:])
    ).astype(low)
    two_out_ref[:, width:] = (
        dot(gate_grad, gate_map_ref[...]) + dot(up_grad, up_map_ref[...])
    ).astype(low)
    down_out_ref[:, :width] = dot(activated, down_ref[...]).astype(low)
    down_out_ref[:, width:] = dot(activated, down_map_ref[...]).astype(low)
    g_gate_ref[...] += dot_tn(mids, gate_grad)
    g_up_ref[...] += dot_tn(mids, up_grad)
    g_down_ref[...] += dot_tn(grad_mid, activated)


def mlp(wide, grad_wide, gate_up, down, gate_map, up_map, down_map):
    span, columns = wide.shape
    hidden = down.shape[0]
    rows = 256
    block = pl.BlockSpec((rows, columns), lambda i: (i, 0))
    grads = jax.ShapeDtypeStruct((EXTRA, hidden), jnp.float32)
    return pl.pallas_call(
        mlp_kernel,
        grid=(span // rows,),
        in_specs=[block, block]
        + [whole(x.shape) for x in (gate_up, down, gate_map, up_map, down_map)],
        out_specs=[block, block] + [kept_out((EXTRA, hidden))] * 3,
        out_shape=[jax.ShapeDtypeStruct((span, columns), low)] * 2 + [grads] * 3,
        compiler_params=pltpu.CompilerParams(vmem_limit_bytes=56 << 20),
        cost_estimate=pl.CostEstimate(
            flops=12 * span * columns * hidden,
            bytes_accessed=8 * span * columns + 6 * hidden * columns,
            transcendentals=span * hidden,
        ),
        name="mlp",
    )(wide, grad_wide, gate_up, down, gate_map, up_map, down_map)


def spread_columns(piece, first):
    return jnp.pad(piece, ((0, 0), (first, EXTRA - first - piece.shape[1])))


def pick_columns(table, adapter, blocks):
    width = ADAPTER_COUNT * RANK
    return jnp.concatenate(
        [
            lax.dynamic_slice_in_dim(table[:, j * width : (j + 1) * width], adapter * RANK, RANK, 1)
            for j in range(blocks)
        ],
        axis=1,
    )


def widen(*parts):
    rows = parts[0].shape[0]
    used = sum(part.shape[1] for part in parts[1:])
    return jnp.concatenate([*parts, jnp.zeros((rows, EXTRA - used), parts[0].dtype)], axis=1)


def gather_rows(rows):
    return lax.all_gather(rows, "shard", axis=0, tiled=True)


def scatter_rows(rows):
    return lax.psum_scatter(rows, "shard", scatter_dimension=0, tiled=True)


def per_device(
    tokens,
    lengths,
    slot_adapter_index,
    norm_gain_rows,
    norm_shift_rows,
    query_key_value_weight,
    query_key_value_bias,
    output_projection_weight,
    gate_up_projection,
    down_projection_weight,
    attention_adapter_input,
    attention_adapter_output,
    output_adapter_input,
    output_adapter_output,
    feedforward_adapter_input,
    feedforward_adapter_output,
    down_adapter_input,
    down_adapter_output,
    output_cotangent,
):
    slot_count, local_span, width = tokens.shape
    shards = lax.axis_size("shard")
    reps = lax.axis_size("rep")
    me = lax.axis_index("shard")
    span = local_span * shards
    own = width // shards
    hidden = gate_up_projection.shape[0]
    places = me * local_span + jnp.arange(local_span, dtype=jnp.int32)
    slots = range(slot_count)
    adapters = [slot_adapter_index[s] for s in slots]

    map_pieces = []
    for s in slots:
        a = adapters[s]
        rows_of = lambda table: lax.dynamic_slice_in_dim(table, a * RANK, RANK, 0).T
        map_pieces += [
            pick_columns(attention_adapter_input, a, 3),
            pick_columns(feedforward_adapter_input, a, 2),
            pick_columns(output_adapter_input, a, 1),
            rows_of(output_adapter_output),
            rows_of(down_adapter_output),
        ]
    maps = gather_rows(jnp.concatenate(map_pieces, axis=1)).reshape(width, slot_count, -1)

    weight_here = lax.all_to_all(
        query_key_value_weight.reshape(own, 3, shards, own), "shard", 2, 0, tiled=True
    ).reshape(width, 3 * own)
    bias_here = lax.dynamic_slice_in_dim(
        query_key_value_bias.reshape(3, width), me * own, own, 1
    ).reshape(1, 3 * own)
    output_full = gather_rows(output_projection_weight)
    tables = rotary_tables(span, own // HEAD_DIM)
    gate_up = gate_up_projection.reshape(hidden, 2 * width)

    kept = []
    for s in slots:
        a = adapters[s]
        own_maps = maps[:, s]
        qkv_in, mlp_in = (own_maps[:, :48], own_maps[:, 48:80])
        out_in, out_out, down_out = (own_maps[:, 80:96], own_maps[:, 96:112], own_maps[:, 112:128])
        valid = (places < lengths[s]).astype(jnp.float32)[:, None]
        inputs = tokens[s].astype(jnp.float32)
        grad_rows = output_cotangent[s].astype(jnp.float32) * valid
        grad_low = grad_rows.astype(low)
        down_mid_grad = (adapter_scale * dot(grad_low, down_out)).astype(low)
        normed, unit_one, inverse_one = layer_norm(inputs, norm_gain_rows[0], norm_shift_rows[0])
        normed = normed.astype(low)
        qkv_mid = dot(normed, qkv_in).astype(low)
        qkv_out = lax.dynamic_slice_in_dim(attention_adapter_output, a * RANK, RANK, 1) * low(2)
        mlp_out = lax.dynamic_slice_in_dim(feedforward_adapter_output, a * RANK, RANK, 2) * low(2)
        kept.append(
            dict(
                qkv_in=qkv_in,
                mlp_in=mlp_in,
                out_in=out_in,
                out_out=out_out,
                down_out=down_out,
                valid=valid,
                inputs=inputs,
                grad_rows=grad_rows,
                grad_low=grad_low,
                down_mid_grad=down_mid_grad,
                normed=normed,
                unit_one=unit_one,
                inverse_one=inverse_one,
                qkv_mid=qkv_mid,
                qkv_map=jnp.concatenate(
                    [
                        jnp.pad(qkv_out[j], ((j * RANK, EXTRA - (j + 1) * RANK), (0, 0)))
                        for j in range(3)
                    ],
                    axis=1,
                ),
                gate_map=spread_columns(mlp_out[:, 0], 0),
                up_map=spread_columns(mlp_out[:, 1], RANK),
                down_map=spread_columns(
                    lax.dynamic_slice_in_dim(down_adapter_input, a * RANK, RANK, 1), 0
                ),
            )
        )

    for s in slots:
        k = kept[s]
        k["wide"] = gather_rows(widen(k["normed"], k["qkv_mid"]))
        k["q"], k["k"], k["v"], k["attended_low"], k["attended"], k["lse"] = attend(
            lengths, k["wide"], weight_here, k["qkv_map"], bias_here, tables, s
        )

    for s in slots:
        k = kept[s]
        attended = lax.all_to_all(k["attended_low"], "shard", 0, 1, tiled=True)
        out_mid = dot(attended, k["out_in"]).astype(low)
        hidden_in = k["inputs"] + (
            dot(attended, output_full) + adapter_scale * dot_nt(out_mid, k["out_out"])
        )
        normed_two, unit_two, inverse_two = layer_norm(
            hidden_in, norm_gain_rows[1], norm_shift_rows[1]
        )
        normed_two = normed_two.astype(low)
        mlp_mid = dot(normed_two, k["mlp_in"]).astype(low)
        k.update(
            attended_rows=attended,
            out_mid=out_mid,
            hidden_in=hidden_in,
            normed_two=normed_two,
            unit_two=unit_two,
            inverse_two=inverse_two,
            mlp_mid=mlp_mid,
        )

    for s in slots:
        k = kept[s]
        wide = gather_rows(widen(k["normed_two"], k["mlp_mid"]))
        grad_wide = gather_rows(widen(k["grad_low"], k["down_mid_grad"]))
        down_partial, two_partial, k["g_gate"], k["g_up"], k["g_down"] = mlp(
            wide,
            grad_wide,
            gate_up,
            down_projection_weight,
            k["gate_map"],
            k["up_map"],
            k["down_map"],
        )
        k["two_sum"] = scatter_rows(two_partial)
        k["down_sum"] = scatter_rows(down_partial)

    for s in slots:
        k = kept[s]
        mlp_mid_grad = k["two_sum"][:, width : width + 2 * RANK]
        two_grad = k["two_sum"][:, :width].astype(jnp.float32) + dot_nt(mlp_mid_grad, k["mlp_in"])
        residual_grad = k["grad_rows"] + layer_norm_back(
            two_grad, k["unit_two"], k["inverse_two"], norm_gain_rows[1]
        )
        branch = residual_grad.astype(low)
        out_mid_grad = (adapter_scale * dot(branch, k["out_out"])).astype(low)
        attended_grad = (dot_nt(branch, output_full) + dot_nt(out_mid_grad, k["out_in"])).astype(
            low
        )
        k.update(
            residual_grad=residual_grad,
            branch=branch,
            mlp_mid_grad=mlp_mid_grad,
            out_mid_grad=out_mid_grad,
        )
        k["head_grad"] = lax.all_to_all(attended_grad, "shard", 1, 0, tiled=True)

    for s in slots:
        k = kept[s]
        one_partial, k["qkv_b"] = attend_back(
            lengths,
            k["q"],
            k["k"],
            k["v"],
            k["lse"],
            k["attended"],
            k["head_grad"],
            k["wide"],
            weight_here,
            k["qkv_map"],
            tables,
            s,
        )
        k["one_sum"] = scatter_rows(one_partial)

    block_parts = []
    token_parts = []
    compact = []
    for s in slots:
        k = kept[s]
        down_mid = k["down_sum"][:, width : width + RANK]
        feed = k["down_sum"][:, :width].astype(jnp.float32) + adapter_scale * dot_nt(
            down_mid, k["down_out"]
        )
        block_parts.append(((k["hidden_in"] + feed) * k["valid"]).astype(low))
        mid_grad = k["one_sum"][:, width : width + 3 * RANK]
        normed_grad = k["one_sum"][:, :width].astype(jnp.float32) + dot_nt(mid_grad, k["qkv_in"])
        token_parts.append(
            k["residual_grad"]
            + layer_norm_back(normed_grad, k["unit_one"], k["inverse_one"], norm_gain_rows[0])
        )
        compact += [
            dot_tn(mid_grad, k["normed"]),
            dot_tn(k["mlp_mid_grad"], k["normed_two"]),
            dot_tn(k["out_mid_grad"], k["attended_rows"]),
            adapter_scale * dot_tn(k["out_mid"], k["branch"]),
            adapter_scale * dot_tn(down_mid, k["grad_low"]),
        ]
    compact = jnp.concatenate(compact, axis=0).astype(low)
    columns = compact.shape[0]
    owned = scatter_rows(
        compact.reshape(columns, shards, own).transpose(1, 0, 2).reshape(shards * columns, own)
    ).reshape(slot_count, 8, RANK, own)

    grads = []
    for s in slots:
        k = kept[s]
        part = [owned[s, j] for j in range(8)]
        part += [
            k["qkv_b"][j * RANK : (j + 1) * RANK, j * own : (j + 1) * own].astype(low)
            for j in range(3)
        ]
        part += [
            (adapter_scale * k["g_gate"][:RANK]).astype(low),
            (adapter_scale * k["g_up"][RANK : 2 * RANK]).astype(low),
            k["g_down"][:RANK].astype(low),
        ]
        grads.append(jnp.concatenate(part, axis=1))
    shared = lax.all_gather(jnp.stack(grads), "rep", axis=0, tiled=True)
    index = lax.all_gather(slot_adapter_index, "rep", axis=0, tiled=True)
    spread = (index[:, None] == jnp.arange(ADAPTER_COUNT, dtype=jnp.int32)[None, :]).astype(
        jnp.float32
    )
    full = jnp.sum(
        shared.astype(jnp.float32)[:, None] * spread[:, :, None, None], axis=0
    ).reshape(ADAPTER_COUNT * RANK, shared.shape[2])
    pieces = [full[:, j * own : (j + 1) * own] for j in range(11)]
    rest = [full[:, 11 * own + j * hidden : 11 * own + (j + 1) * hidden] for j in range(3)]
    return (
        jnp.stack(block_parts),
        jnp.stack(token_parts),
        jnp.concatenate([piece.T for piece in pieces[:3]], axis=1),
        jnp.stack(pieces[8:11]),
        pieces[5].T,
        pieces[6],
        jnp.concatenate([piece.T for piece in pieces[3:5]], axis=1),
        jnp.stack([rest[0].T, rest[1].T], axis=1),
        rest[2].T,
        pieces[7],
    )


def solution(mesh):
    rows = P("shard", None)
    in_specs = (
        P("rep", "shard", None),
        P("rep"),
        P("rep"),
        P(),
        P(),
        rows,
        P(),
        rows,
        P("shard", None, None),
        rows,
        rows,
        P(None, None, "shard"),
        rows,
        P(None, "shard"),
        rows,
        P("shard", None, None),
        rows,
        P(None, "shard"),
        P("rep", "shard", None),
    )
    out_specs = (
        P("rep", "shard", None),
        P("rep", "shard", None),
        rows,
        P(None, None, "shard"),
        rows,
        P(None, "shard"),
        rows,
        P("shard", None, None),
        rows,
        P(None, "shard"),
    )
    return jax.shard_map(
        per_device, mesh=mesh, in_specs=in_specs, out_specs=out_specs, check_vma=False
    )
```

time: 857 us -> 800 us (0.933)
  matrix products: 288 us -> 61.5 us
  waiting for transfers between devices: 246 us -> 415 us
  Pallas kernels: 0 us -> 139 us
  local copies, waits for them, and re-layouts: 194 us -> 80.7 us
  other arithmetic: 70 us -> 32.4 us
  blocking collectives: 9.03 us -> 34.5 us
    pallas_call x0 -> x6, Pallas kernels: none -> 139 us  [the longest x2 62.5 us: mlp(): pl.pallas_call(mlp_kernel, grid=(span // rows,), in_specs=[block, block]...]
    reduce_scatter x7, waiting for transfers between devices: 95.4 us -> 198 us  [scatter_rows(): return lax.psum_scatter(rows, 'shard', scatter_dimension=0, tiled=True)]
    all_gather x8, waiting for transfers between devices: 72.3 us -> 143 us  [gather_rows(): return lax.all_gather(rows, 'shard', axis=0, tiled=True)]
    dot_general x32 -> x12, matrix products: 97.9 us -> 30 us  [dot_nt(): lax.dot_general(a, b, (((1,), (1,)), ((), ())), preferred_element_type=jn...]
    dot_general x13 -> x0, matrix products: 67.7 us -> none  [the longest x2 19.9 us: attend_back(): jnp.einsum('qgd,kgd->gqk', g, v, preferred_element_type=jnp.float32)]
    dot_general x32 -> x12, matrix products: 82.2 us -> 15.4 us  [dot(): return jnp.dot(a, b, preferred_element_type=jnp.float32)]
    concatenate x8 -> x3, local copies, waits for them, and re-layouts: 48.1 us -> 3.26 us  [the longest x2 1.78 us: per_device(): grads.append(jnp.concatenate(part, axis=1))]
    slice x43 -> x6, local copies, waits for them, and re-layouts: 42.8 us -> 4.82 us  [the longest x2 2.82 us: per_device(): k['g_down'][:RANK].astype(low)]
  transfers between devices with their start and end apart: 21 -> 19, of which waited for: 11 -> 15; matrix products, arithmetic and copies ran while one was open for 56% -> 18% of each run, Pallas kernels for 0% -> 18%
where the time goes in v2:
time: 800 us; the launch traced here: 794 us
  waiting for transfers between devices  415 us (52%)
  Pallas kernels  139 us (17%)
  local copies, waits for them, and re-layouts  80.7 us (10%)
  matrix products  61.5 us (8%)
  blocking collectives  34.5 us (4%)
  other arithmetic  32.4 us (4%)
  between operations  17.1 us (2%)
  starting transfers between devices  13.2 us (2%)
    reduce_scatter x7, waiting for transfers between devices, scatter_rows(): return lax.psum_scatter(rows, 'shard', scatter_dimension=0, tiled=True)  198 us
    all_gather x8, waiting for transfers between devices, gather_rows(): return lax.all_gather(rows, 'shard', axis=0, tiled=True)  143 us
    pallas_call x2, Pallas kernels, mlp(): pl.pallas_call(mlp_kernel, grid=(span // rows,), in_specs=[block, block]...  62.5 us
    pallas_call x2, Pallas kernels, attend_back(): pl.pallas_call(lambda *refs: attend_back_kernel(*refs, slot=slot, steps=s...  43.9 us
    all_to_all x1, waiting for transfers between devices, per_device(): lax.all_to_all(query_key_value_weight.reshape(own, 3, shards, own), 'shar...  37.4 us
    pallas_call x2, Pallas kernels, attend(): pl.pallas_call(lambda *refs: attend_kernel(*refs, slot=slot, steps=span /...  32.8 us
    unnamed x115, local copies, waits for them, and re-layouts  32.7 us
    dot_general x12, matrix products, dot_nt(): lax.dot_general(a, b, (((1,), (1,)), ((), ())), preferred_element_type=jn...  30 us
  transfers between devices with their start and end apart: 19, of which 15 were waited for; matrix products, arithmetic and copies ran while one was open for 18% of the time, Pallas kernels for 18%

profile of v2, /device:TPU:0, one launch (start us, length us, event | category | flops | bytes accessed | tf_op | source)
XLA Modules:
  0.0 793.7 jit_solution(8304368970649677611)
XLA Ops:
  20.2 23.8 %all-gather.10.cloned.1.call-done = bf16[2048,256]{0,1:T(8,128)(2,1)} async-done(((bf16[256,256]{0,1:T(8,128)(2,1)}), bf16[2048,256]{0,1:T(8,128)(2,1)}) %all-gather.10.cloned.1.call-update) | async-done | bytes 1048592 | tf_op jit(solution)/shard_map/all_gather | solution.py:383
  48.8 4.6 copy.244
  57.6 4.6 all-to-all-start
  69.5 5.1 fusion.24
  74.5 37.4 %all-to-all-done = bf16[256,3,8,256]{0,3,1,2:T(8,128)(2,1)} async-done(((bf16[256,3,8,256]{0,3,1,2:T(8,128)(2,1)}), bf16[256,3,8,256]{0,3,1,2:T(8,128)(2,1)}, u32[]{:S(2)}, u32[]{:S(2)}) %all-to-all-start) | async-done | bytes 3145760 | tf_op jit(solution)/shard_map/all_to_all | solution.py:435
  111.9 7.3 copy.287
  119.2 4.7 copy.316
  123.9 16.4 %attend.3 = (bf16[1024,256]{1,0:T(8,128)(2,1)}, bf16[1024,256]{1,0:T(8,128)(2,1)}, bf16[1024,256]{1,0:T(8,128)(2,1)}, bf16[1024,256]{1,0:T(8,128)(2,1)}, f32[1024,256]{1,0:T(8,128)}, /*index=5*/f32[1024,128]{1,0:T(8,128)}) custom-call(s32[2]{0:T(128)} %refs_0_.7, bf16[1024,2176]{1,0:T(8,128)(2,1)} %all-gather.20.cloned.1.call-done.refs_1_.refs_7_, ...), custom_call_target="tpu_custom_call" | custom-call | flops 7717519360 | bytes 7602176 | tf_op jit(solution)/shard_map/attend/pallas_call | solution.py:155
  147.6 16.4 %attend.2 = (bf16[1024,256]{1,0:T(8,128)(2,1)}, bf16[1024,256]{1,0:T(8,128)(2,1)}, bf16[1024,256]{1,0:T(8,128)(2,1)}, bf16[1024,256]{1,0:T(8,128)(2,1)}, f32[1024,256]{1,0:T(8,128)}, /*index=5*/f32[1024,128]{1,0:T(8,128)}) custom-call(s32[2]{0:T(128)} %refs_0_.7, bf16[1024,2176]{1,0:T(8,128)(2,1)} %all-gather.12.cloned.1.call-done.refs_1_.refs_7_, ...), custom_call_target="tpu_custom_call" | custom-call | flops 7717519360 | bytes 7602176 | tf_op jit(solution)/shard_map/attend/pallas_call | solution.py:155
  170.6 8.6 %all-to-all-done.1 = bf16[8,128,256]{1,2,0:T(8,128)(2,1)S(1)} async-done(((bf16[8,128,256]{1,2,0:T(8,128)(2,1)}), bf16[8,128,256]{1,2,0:T(8,128)(2,1)S(1)}, u32[]{:S(2)}, u32[]{:S(2)}) %all-to-all-start.1) | async-done | bytes 524320 | tf_op jit(solution)/shard_map/all_to_all | solution.py:501
  180.2 23.4 %all-gather.14.cloned.1.call-done = bf16[2048,2048]{1,0:T(8,128)(2,1)} async-done(((bf16[256,2048]{1,0:T(8,128)(2,1)}), bf16[2048,2048]{1,0:T(8,128)(2,1)}) %all-gather.14.cloned.1.call-update) | async-done | bytes 8388624 | tf_op jit(solution)/shard_map/all_gather | solution.py:383
  203.6 4.8 fusion.145
  221.9 8.9 %copy.318 = bf16[88,8,2,2048]{3,1,2,0:T(8,128)(2,1)} copy(bf16[88,8,2,2048]{3,2,1,0:T(2,128)(2,1)} %bitcast.307) | data formatting | bytes 11534336
  234.2 8.7 %all-gather.18.cloned.1.call-done.grad_ref = bf16[1024,2176]{1,0:T(8,128)(2,1)} async-done(((bf16[128,2176]{1,0:T(8,128)(2,1)}), bf16[1024,2176]{1,0:T(8,128)(2,1)}) %all-gather.18.cloned.1.call-update) | async-done | bytes 4456464 | tf_op jit(solution)/shard_map/all_gather | solution.py:383
  243.0 39.5 %all-gather.16.cloned.1.call-done.wide_ref = bf16[1024,2176]{1,0:T(8,128)(2,1)} async-done(((bf16[128,2176]{1,0:T(8,128)(2,1)}), bf16[1024,2176]{1,0:T(8,128)(2,1)}) %all-gather.16.cloned.1.call-update) | async-done | bytes 4456464 | tf_op jit(solution)/shard_map/all_gather | solution.py:383
  282.4 31.2 %mlp.2 = (bf16[1024,2176]{1,0:T(8,128)(2,1)}, bf16[1024,2176]{1,0:T(8,128)(2,1)}, f32[128,704]{1,0:T(8,128)}, f32[128,704]{1,0:T(8,128)}, f32[128,704]{1,0:T(8,128)}) custom-call(bf16[1024,2176]{1,0:T(8,128)(2,1)} %all-gather.16.cloned.1.call-done.wide_ref, bf16[1024,2176]{1,0:T(8,128)(2,1)} %all-gather.18.cloned.1.call-done.grad_ref, ...), custom_call_target="tpu_custom_call" | custom-call | flops 18824036352 | bytes 27017216 | tf_op jit(solution)/shard_map/mlp/pallas_call | solution.py:344
  316.2 5.9 all-gather.24.cloned.1.call-done.grad_ref
  322.0 40.2 %all-gather.22.cloned.1.call-done.wide_ref = bf16[1024,2176]{1,0:T(8,128)(2,1)} async-done(((bf16[128,2176]{1,0:T(8,128)(2,1)}), bf16[1024,2176]{1,0:T(8,128)(2,1)}) %all-gather.22.cloned.1.call-update) | async-done | bytes 4456464 | tf_op jit(solution)/shard_map/all_gather | solution.py:383
  362.2 31.2 %mlp.3 = (bf16[1024,2176]{1,0:T(8,128)(2,1)}, bf16[1024,2176]{1,0:T(8,128)(2,1)}, f32[128,704]{1,0:T(8,128)}, f32[128,704]{1,0:T(8,128)}, f32[128,704]{1,0:T(8,128)}) custom-call(bf16[1024,2176]{1,0:T(8,128)(2,1)} %all-gather.22.cloned.1.call-done.wide_ref, bf16[1024,2176]{1,0:T(8,128)(2,1)} %all-gather.24.cloned.1.call-done.grad_ref, ...), custom_call_target="tpu_custom_call" | custom-call | flops 18824036352 | bytes 27017216 | tf_op jit(solution)/shard_map/mlp/pallas_call | solution.py:344
  394.8 23.4 %reduce-scatter.12.cloned.1.call-done = bf16[128,2176]{1,0:T(8,128)(2,1)} async-done(((bf16[1024,2176]{1,0:T(8,128)(2,1)}), bf16[128,2176]{1,0:T(8,128)(2,1)}) %reduce-scatter.12.cloned.1.call-update) | async-done | bytes 557072 | tf_op jit(solution)/shard_map/reduce_scatter | solution.py:387
  420.7 53.4 %reduce-scatter.16.cloned.1.call-done = bf16[128,2176]{1,0:T(8,128)(2,1)} async-done(((bf16[1024,2176]{1,0:T(8,128)(2,1)}), bf16[128,2176]{1,0:T(8,128)(2,1)}) %reduce-scatter.16.cloned.1.call-update) | async-done | bytes 557072 | tf_op jit(solution)/shard_map/reduce_scatter | solution.py:387
  480.1 6.6 fusion.129
  488.0 13.0 %all_to_all.91 = bf16[128,8,256]{2,0,1:T(8,128)(2,1)} all-to-all(bf16[128,8,256]{2,0,1:T(8,128)(2,1)S(1)} %bitcast.318), channel_id=1, replica_groups=mesh['shard'=8,'rep'=4] {'shard'}, dimensions={1} | all-to-all | bytes 1048576 | tf_op jit(solution)/shard_map/all_to_all | solution.py:555
  501.0 21.9 %attend_back.2 = (bf16[1024,2176]{1,0:T(8,128)(2,1)}, f32[128,768]{1,0:T(8,128)}) custom-call(s32[2]{0:T(128)} %refs_0_.7, bf16[1024,256]{1,0:T(8,128)(2,1)} %get-tuple-element.41.refs_1_, bf16[1024,256]{1,0:T(8,128)(2,1)} %get-tuple-element.42.refs_2_, bf16[1024,256]{1,0:T(8,128)(2,1)} %get-tuple-element.43.refs_3_, f32[1024,128]{1,0:T(8,128)} %get-tuple-element.44.refs_4_, ...), custom_call_target="tpu_custom_call" | custom-call | flops 13958643712 | bytes 7340032 | tf_op jit(solution)/shard_map/attend_back/pallas_call | solution.py:267
  524.4 6.7 fusion.125
  532.4 13.2 %all_to_all.92 = bf16[128,8,256]{2,0,1:T(8,128)(2,1)} all-to-all(bf16[128,8,256]{2,0,1:T(8,128)(2,1)S(1)} %bitcast.319), channel_id=1, replica_groups=mesh['shard'=8,'rep'=4] {'shard'}, dimensions={1} | all-to-all | bytes 1048576 | tf_op jit(solution)/shard_map/all_to_all | solution.py:555
  545.6 22.0 %attend_back.3 = (bf16[1024,2176]{1,0:T(8,128)(2,1)}, f32[128,768]{1,0:T(8,128)}) custom-call(s32[2]{0:T(128)} %refs_0_.7, bf16[1024,256]{1,0:T(8,128)(2,1)} %get-tuple-element.48.refs_1_, bf16[1024,256]{1,0:T(8,128)(2,1)} %get-tuple-element.49.refs_2_, bf16[1024,256]{1,0:T(8,128)(2,1)} %get-tuple-element.50.refs_3_, f32[1024,128]{1,0:T(8,128)} %get-tuple-element.51.refs_4_, ...), custom_call_target="tpu_custom_call" | custom-call | flops 13958643712 | bytes 7340032 | tf_op jit(solution)/shard_map/attend_back/pallas_call | solution.py:267
  569.8 8.2 %all-reduce.12 = s32[8]{0:T(128)S(1)} all-reduce(s32[8]{0:T(128)S(1)} %dynamic-update-slice), channel_id=1, replica_groups=mesh['shard'=8,'rep'=4] {'rep'}, use_global_device_ids=true, to_apply=%add.12 | all-reduce | flops 8 | bytes 64
  593.7 48.5 %reduce-scatter.14.cloned.1.call-done = bf16[128,2176]{1,0:T(8,128)(2,1)} async-done(((bf16[1024,2176]{1,0:T(8,128)(2,1)}), bf16[128,2176]{1,0:T(8,128)(2,1)}) %reduce-scatter.14.cloned.1.call-update) | async-done | bytes 557072 | tf_op jit(solution)/shard_map/reduce_scatter | solution.py:387
  648.1 50.0 %reduce-scatter.18.cloned.1.call-done = bf16[128,2176]{1,0:T(8,128)(2,1)} async-done(((bf16[1024,2176]{1,0:T(8,128)(2,1)}), bf16[128,2176]{1,0:T(8,128)(2,1)}) %reduce-scatter.18.cloned.1.call-update) | async-done | bytes 557072 | tf_op jit(solution)/shard_map/reduce_scatter | solution.py:387
  719.7 22.2 %reduce-scatter.20.cloned.1.call-done = bf16[256,256]{1,0:T(8,128)(2,1)} async-done(((bf16[2048,256]{1,0:T(8,128)(2,1)}), bf16[256,256]{1,0:T(8,128)(2,1)}) %reduce-scatter.20.cloned.1.call-update) | async-done | bytes 131088 | tf_op jit(solution)/shard_map/reduce_scatter | solution.py:387
  750.7 26.8 %all-gather.26.cloned.1.call-done = bf16[8,16,4928]{2,1,0:T(8,128)(2,1)} async-done(((bf16[2,16,4928]{2,1,0:T(8,128)(2,1)}), bf16[8,16,4928]{2,1,0:T(8,128)(2,1)}) %all-gather.26.cloned.1.call-update) | async-done | bytes 1261584 | tf_op jit(solution)/shard_map/all_gather | solution.py:618
  (284 shorter events, 138.0 us)
Async XLA Ops:
  7.2 36.8 %all-gather.10.cloned.1.call-start = ((), (), s32[]{:S(2)}) async-start(), calls=%async_computation.12 | async-start | bytes 1179648 | tf_op jit(solution)/shard_map/all_gather | solution.py:383
  17.6 106.2 %all-gather.20.cloned.1.call-start = ((), (), s32[]{:S(2)}) async-start(), calls=%async_computation.18 | async-start | bytes 5013504 | tf_op jit(solution)/shard_map/all_gather | solution.py:383
  19.1 26.2 %copy-start.25 = (f32[128]{0:T(128)}, f32[128]{0:T(128)S(1)}, u32[]{:S(2)}) copy-start(f32[128]{0:T(128)S(1)} %get-tuple-element.233) | copy-start | bytes 1540
  19.1 26.2 %copy-start.26 = (f32[128]{0:T(128)}, f32[128]{0:T(128)S(1)}, u32[]{:S(2)}) copy-start(f32[128]{0:T(128)S(1)} %get-tuple-element.234) | copy-start | bytes 1540
  20.1 33.3 %copy-start.6 = (bf16[128,2048]{1,0:T(8,128)(2,1)}, bf16[128,2048]{1,0:T(8,128)(2,1)S(1)}, u32[]{:S(2)}) copy-start(bf16[128,2048]{1,0:T(8,128)(2,1)S(1)} %get-tuple-element.149) | copy-start | bytes 1572868
  20.2 33.3 %copy-start.7 = (bf16[128,2048]{1,0:T(8,128)(2,1)}, bf16[128,2048]{1,0:T(8,128)(2,1)S(1)}, u32[]{:S(2)}) copy-start(bf16[128,2048]{1,0:T(8,128)(2,1)S(1)} %get-tuple-element.148) | copy-start | bytes 1572868
  46.8 100.8 %all-gather.12.cloned.1.call-start = ((), (), s32[]{:S(2)}) async-start(), calls=%async_computation.13 | async-start | bytes 5013504 | tf_op jit(solution)/shard_map/all_gather | solution.py:383
  48.2 155.4 %all-gather.14.cloned.1.call-start = ((), (), s32[]{:S(2)}) async-start(), calls=%async_computation.14 | async-start | bytes 9437184 | tf_op jit(solution)/shard_map/all_gather | solution.py:383
  57.6 54.4 %all-to-all-start = ((bf16[256,3,8,256]{0,3,1,2:T(8,128)(2,1)}), bf16[256,3,8,256]{0,3,1,2:T(8,128)(2,1)}, u32[]{:S(2)}, u32[]{:S(2)}) async-start(bf16[256,3,8,256]{0,3,1,2:T(8,128)(2,1)} %copy.245), calls=%async_computation | async-start | bytes 6291456 | tf_op jit(solution)/shard_map/all_to_all | solution.py:435
  62.2 180.8 %all-gather.18.cloned.1.call-start = ((), (), s32[]{:S(2)}) async-start(), calls=%async_computation.16 | async-start | bytes 5013504 | tf_op jit(solution)/shard_map/all_gather | solution.py:383
  64.3 411.5 %copy-start.27 = (f32[128]{0:T(128)}, f32[128]{0:T(128)S(1)}, u32[]{:S(2)}) copy-start(f32[128]{0:T(128)S(1)} %get-tuple-element.247) | copy-start | bytes 1540
  64.3 411.5 %copy-start.29 = (f32[128]{0:T(128)}, f32[128]{0:T(128)S(1)}, u32[]{:S(2)}) copy-start(f32[128]{0:T(128)S(1)} %get-tuple-element.246) | copy-start | bytes 1540
  65.3 53.9 %copy-start.10 = (bf16[128,2048]{1,0:T(8,128)(2,1)}, bf16[128,2048]{1,0:T(8,128)(2,1)S(1)}, u32[]{:S(2)}) copy-start(bf16[128,2048]{1,0:T(8,128)(2,1)S(1)} %get-tuple-element.154) | copy-start | bytes 1572868
  142.3 23.7 %all-to-all-start.2 = ((bf16[8,128,256]{1,2,0:T(8,128)(2,1)}), bf16[8,128,256]{1,2,0:T(8,128)(2,1)S(1)}, u32[]{:S(2)}, u32[]{:S(2)}) async-start(bf16[8,128,256]{1,2,0:T(8,128)(2,1)} %copy.255), calls=%async_computation.3 | async-start | bytes 1048576 | tf_op jit(solution)/shard_map/all_to_all | solution.py:501
  166.0 44.0 %copy-start.4 = (bf16[8,128,256]{1,2,0:T(8,128)(2,1)}, bf16[8,128,256]{1,2,0:T(8,128)(2,1)S(1)}, u32[]{:S(2)}) copy-start(bf16[8,128,256]{1,2,0:T(8,128)(2,1)S(1)} %all-to-all-done.2) | copy-start | bytes 1572868
  166.0 13.1 %all-to-all-start.1 = ((bf16[8,128,256]{1,2,0:T(8,128)(2,1)}), bf16[8,128,256]{1,2,0:T(8,128)(2,1)S(1)}, u32[]{:S(2)}, u32[]{:S(2)}) async-start(bf16[8,128,256]{1,2,0:T(8,128)(2,1)} %copy.248), calls=%async_computation.1 | async-start | bytes 1048576 | tf_op jit(solution)/shard_map/all_to_all | solution.py:501
  169.5 112.9 %all-gather.16.cloned.1.call-start = ((), (), s32[]{:S(2)}) async-start(), calls=%async_computation.15 | async-start | bytes 5013504 | tf_op jit(solution)/shard_map/all_gather | solution.py:383
  179.2 29.3 %copy-start.5 = (bf16[8,128,256]{1,2,0:T(8,128)(2,1)}, bf16[8,128,256]{1,2,0:T(8,128)(2,1)S(1)}, u32[]{:S(2)}) copy-start(bf16[8,128,256]{1,2,0:T(8,128)(2,1)S(1)} %all-to-all-done.1) | copy-start | bytes 1572868
  215.9 106.2 %all-gather.24.cloned.1.call-start = ((), (), s32[]{:S(2)}) async-start(), calls=%async_computation.20 | async-start | bytes 5013504 | tf_op jit(solution)/shard_map/all_gather | solution.py:383
  219.1 143.1 %all-gather.22.cloned.1.call-start = ((), (), s32[]{:S(2)}) async-start(), calls=%async_computation.19 | async-start | bytes 5013504 | tf_op jit(solution)/shard_map/all_gather | solution.py:383
  221.5 196.8 %reduce-scatter.12.cloned.1.call-start = ((), (), s32[]{:S(2)}) async-start(), calls=%async_computation.22 | async-start | bytes 5013504 | tf_op jit(solution)/shard_map/reduce_scatter | solution.py:387
  313.7 160.4 %reduce-scatter.16.cloned.1.call-start = ((), (), s32[]{:S(2)}) async-start(), calls=%async_computation.24 | async-start | bytes 5013504 | tf_op jit(solution)/shard_map/reduce_scatter | solution.py:387
  393.5 192.1 %reduce-scatter.8.cloned.1.call-start = ((), (), s32[]{:S(2)}) async-start(), calls=%async_computation.17 | async-start | bytes 5013504 | tf_op jit(solution)/shard_map/reduce_scatter | solution.py:387
  394.2 192.7 %reduce-scatter.10.cloned.1.call-start = ((), (), s32[]{:S(2)}) async-start(), calls=%async_computation.21 | async-start | bytes 5013504 | tf_op jit(solution)/shard_map/reduce_scatter | solution.py:387
  394.8 247.4 %reduce-scatter.14.cloned.1.call-start = ((), (), s32[]{:S(2)}) async-start(), calls=%async_computation.23 | async-start | bytes 5013504 | tf_op jit(solution)/shard_map/reduce_scatter | solution.py:387
  522.9 175.2 %reduce-scatter.18.cloned.1.call-start = ((), (), s32[]{:S(2)}) async-start(), calls=%async_computation.25 | async-start | bytes 5013504 | tf_op jit(solution)/shard_map/reduce_scatter | solution.py:387
  567.7 174.2 %reduce-scatter.20.cloned.1.call-start = ((), (), s32[]{:S(2)}) async-start(), calls=%async_computation.26 | async-start | bytes 1179648 | tf_op jit(solution)/shard_map/reduce_scatter | solution.py:387
  591.6 121.3 %copy-start.28 = (f32[128]{0:T(128)S(1)}, f32[128]{0:T(128)}, u32[]{:S(2)}) copy-start(f32[128]{0:T(128)} %copy-done.27) | copy-start | bytes 1540
  705.8 71.7 %all-gather.26.cloned.1.call-start = ((), (), s32[]{:S(2)}) async-start(), calls=%async_computation.27 | async-start | bytes 1597440 | tf_op jit(solution)/shard_map/all_gather | solution.py:618
  712.9 32.4 %copy-start.3 = (bf16[2,128,2048]{2,1,0:T(8,128)(2,1)S(1)}, bf16[2,128,2048]{2,1,0:T(8,128)(2,1)}, u32[]{:S(2)}) copy-start(bf16[2,128,2048]{2,1,0:T(8,128)(2,1)} %param.19) | copy-start | bytes 3145732
  715.5 32.2 %copy-start.1 = (f32[128,2048]{1,0:T(8,128)S(1)}, f32[128,2048]{1,0:T(8,128)}, u32[]{:S(2)}) copy-start(f32[128,2048]{1,0:T(8,128)} %get-tuple-element.153) | copy-start | bytes 3145732
  749.2 29.8 %copy-start.24 = (f32[8,8]{1,0:T(8,128)S(1)}, f32[8,8]{1,0:T(8,128)}, u32[]{:S(2)}) copy-start(f32[8,8]{1,0:T(8,128)} %fusion.118) | copy-start | bytes 772
  (22 other events, 223.5 us)
Sparse Core Ops, SparseCore 0:
  17.8 26.1 all-gather.9
  46.9 57.2 all-gather.19
  106.1 41.4 all-gather.11
  149.3 54.2 all-gather.13
  205.4 37.5 all-gather.17
  244.7 37.6 all-gather.15
  284.3 37.6 all-gather.23
  324.5 37.6 all-gather.21
  365.7 52.5 reduce-scatter.11
  421.5 52.5 reduce-scatter.15
  477.6 52.5 reduce-scatter.7
  533.5 52.5 reduce-scatter.9
  589.5 52.5 reduce-scatter.13
  645.5 52.5 reduce-scatter.17
  705.9 35.9 reduce-scatter.19
  745.5 31.9 all-gather.25
